TPU v7x, 128 devices: a whole 4x4x4 slice. The times are simulated.
128 devices in a mesh: dp: 8 (over x_lo, z), tensor: 16 (over x_hi, y, core).
Axes of the slice: x: 4 (x_hi: 2, x_lo: 2; x = x_hi * 2 + x_lo), y: 4, z: 4, core: 2. Of those that a mesh axis runs over, the one named last changes fastest.
Arguments:
- tokens: bfloat16 [4096, 4096], P('dp', 'tensor'), may hold values from -6 to 6
- cotangent: bfloat16 [4096, 4096], P('dp', 'tensor'), may hold values from -6 to 6
- gate_weight: bfloat16 [4096, 14336], P('dp', 'tensor'), may hold values from -0.09375 to 0.09375
- up_weight: bfloat16 [4096, 14336], P('dp', 'tensor'), may hold values from -0.09375 to 0.09375
- down_weight: bfloat16 [4096, 14336], P('dp', 'tensor'), may hold values from -0.046875 to 0.046875
- gate_keep: int32 [32, 112], P('dp', 'tensor'), may hold values from 0 to 1, as said below
- up_keep: int32 [32, 112], P('dp', 'tensor'), may hold values from 0 to 1, as said below
- down_keep: int32 [32, 112], P('dp', 'tensor'), may hold values from 0 to 1, as said below
Outputs:
- grad_tokens: bfloat16 [4096, 4096], P('dp', 'tensor')
- grad_gate: bfloat16 [4096, 14336], P('dp', 'tensor')
- grad_up: bfloat16 [4096, 14336], P('dp', 'tensor')
- grad_down: bfloat16 [4096, 14336], P('dp', 'tensor')
Inputs may be any that keep to these rules, and one draw needn't show every extreme that they name: `gate_keep`: 1 keeps the 128 x 128 tile of the gate projection, 0 prunes it; the kept share of each range of 7 tile columns held by one device of tensor lies between 0.25 and 0.75 in expectation and differs between ranges; any 0/1 mask is allowed, and no bound on the number of kept tiles in a device's [4, 7] block is promised. `up_keep`: as for gate_keep, for the up projection. `down_keep`: as for gate_keep, for the down projection.
All inputs are finite; a program needn't handle non-finite values.
Results may differ from a plain program's by a relative error of at most 0.018.
Values may be sent and summed in bfloat16 or wider, within the bound.
No kernel may reach another device: no remote copies, remote signals or barrier semaphores. Data moves between devices by JAX's collectives and lax.ppermute only.
A program may use at most 192 MiB of HBM per device.

v0:
```python
import jax
import jax.numpy as jnp
from jax import lax
from jax.experimental import pallas as pl
from jax.experimental.pallas import tpu as pltpu
from jax.sharding import Mesh
from jax.sharding import PartitionSpec as P


F32 = jnp.float32
BF16 = jnp.bfloat16
X = ("xl", "xh")
VMEM_LIMIT = 56 * 1024 * 1024
NT = (((1,), (1,)), ((), ()))
NN = (((1,), (0,)), ((), ()))
RANGE = 448
TOKENS = 1024


def shift(value, axis, size, step):
    name = (lambda i: i % 2 * 2 + i // 2) if axis == X else (lambda i: i)
    return lax.ppermute(value, axis, [(name(i), name((i + step) % size)) for i in range(size)])


def expand(tile_keep):
    row_tiles, col_tiles = tile_keep.shape
    spread = jnp.broadcast_to(tile_keep[:, None, :, None], (row_tiles, 128, col_tiles, 128))
    return spread.reshape(row_tiles * 128, col_tiles * 128)


def gather_four(block, axis):
    return jnp.stack([block] + [shift(block, axis, 4, -d) for d in (1, 2, 3)])


def send_four(pieces, axis):
    return [pieces[0]] + [shift(pieces[d], axis, 4, d) for d in (1, 2, 3)]


def ring_gather(block):
    left, right = shift(block, "z", 4, 1), shift(block, "z", 4, -1)
    cut = (2, block.shape[0] * block.shape[1] // 2, block.shape[2])
    across = jnp.stack(
        [shift(left.reshape(cut)[0], "z", 4, 1), shift(right.reshape(cut)[1], "z", 4, -1)]
    )
    return jnp.stack([block, right, across.reshape(block.shape), left])


def ring_scatter(pieces):
    own, right, across, left = (pieces[d] for d in range(4))
    low, high = shift(across[0], "z", 4, 1), shift(across[1], "z", 4, -1)
    right_0, right_1, left_0, left_1 = right[0], right[1], left[0], left[1]
    right_0, left_1 = total_of((right_0, low)), total_of((left_1, high))
    to_right, to_left = jnp.stack([right_0, right_1]), jnp.stack([left_0, left_1])
    return [own, shift(to_right, "z", 4, 1), shift(to_left, "z", 4, -1)]


def total_of(blocks):
    return sum(b.astype(F32) for b in blocks).astype(BF16)


def turn_x(pos, xh, xl):
    return lax.rem(xh * 2 + xl + 4 - pos[0], 4)


def turn_y(pos, y):
    return lax.rem(y + 4 - pos[1], 4)


def act_specs(far_of, x_first):
    def spec(xl):
        def place(s, pos):
            z, far = far_of(s)
            turned = (turn_y(pos, z), turn_x(pos, far ^ pos[3], xl))
            return (turned[::-1] if x_first else turned) + (0, 0)

        return pl.BlockSpec((1, 1, 512, 256), place)

    return [spec(0), spec(0), spec(1), spec(1)]


def whole(shape):
    return pl.BlockSpec(shape, lambda *ids: (0,) * len(shape))


def by_z(count, first):
    return pl.BlockSpec((1, count, RANGE, 512), lambda s, *rest: (s, first, 0, 0))


def by_turned_z(count, first):
    def place(s, *rest):
        return (lax.rem(s + 4 - rest[-1][4], 4), first, 0, 0)

    return pl.BlockSpec((1, count, RANGE, 512), place)


def call(kernel, steps, in_specs, outs, out_specs, scratch, flops, args):
    moved = sum(a.size * a.dtype.itemsize for a in args)
    return pl.pallas_call(
        kernel,
        out_shape=[jax.ShapeDtypeStruct(shape, kind) for shape, kind in outs],
        grid_spec=pltpu.PrefetchScalarGridSpec(
            num_scalar_prefetch=1,
            grid=steps,
            in_specs=in_specs,
            out_specs=out_specs,
            scratch_shapes=scratch,
        ),
        compiler_params=pltpu.CompilerParams(vmem_limit_bytes=VMEM_LIMIT),
        cost_estimate=pl.CostEstimate(flops=flops, bytes_accessed=moved, transcendentals=0),
    )(*args)


FLOPS = 2 * RANGE * TOKENS * 4096
SUMS = (RANGE, TOKENS)
PAIR = (2 * RANGE, TOKENS)


def core_columns(pos):
    own = pl.ds(pl.multiple_of(pos[2] * 256, 256), 256)
    other = pl.ds(pl.multiple_of((1 - pos[2]) * 256, 256), 256)
    return own, other


def own_first(pos, w):
    own, other = core_columns(pos)
    return jnp.concatenate([w[:, own], w[:, other]], axis=1)


def beside(own_ref, other_ref):
    return jnp.concatenate([own_ref[0, 0], other_ref[0, 0]], axis=1)


HALVES = (slice(0, 512), slice(512, 1024))


def near_sums_kernel(pos, w_ref, a0, b0, a1, b1, sums_ref):
    first = pl.program_id(0) == 0
    w = own_first(pos, w_ref.at[0].reshape(2 * RANGE, 512))
    for cols, (own, other) in zip(HALVES, ((a0, b0), (a1, b1))):
        term = lax.dot_general(w, beside(own, other), NT, preferred_element_type=F32)

        @pl.when(first)
        def _():
            sums_ref[:, cols] = term

        @pl.when(jnp.logical_not(first))
        def _():
            sums_ref[:, cols] += term


def far_sums_kernel(pos, w_ref, a0, b0, a1, b1, near_ref, sums_ref, hidden_ref):
    first = pl.program_id(0) == 0
    w = own_first(pos, w_ref.at[0].reshape(2 * RANGE, 512))
    for cols, (own, other) in zip(HALVES, ((a0, b0), (a1, b1))):
        term = lax.dot_general(w, beside(own, other), NT, preferred_element_type=F32)

        @pl.when(first)
        def _():
            sums_ref[:, cols] = near_ref[:, cols] + term

        @pl.when(jnp.logical_not(first))
        def _():
            sums_ref[:, cols] += term

    @pl.when(pl.program_id(0) == 3)
    def _():
        @pl.loop(0, RANGE // 16)
        def _(i):
            gate = sums_ref[pl.ds(i * 16, 16), :]
            up = sums_ref[pl.ds(RANGE + i * 16, 16), :]
            hidden_ref[pl.ds(i * 16, 16), :] = (gate * jax.nn.sigmoid(gate) * up).astype(BF16)


def hidden_grad_kernel(
    pos, near_ref, far_ref, a0, b0, a1, b1, c0, d0, c1, d1, sums_ref, grads_ref, turned_ref, acc
):
    first = pl.program_id(0) == 0
    near, far = own_first(pos, near_ref.at[0, 0]), own_first(pos, far_ref.at[0, 0])
    for cols, pairs in zip(HALVES, ((a0, b0, c0, d0), (a1, b1, c1, d1))):
        term = lax.dot_general(near, beside(*pairs[:2]), NT, preferred_element_type=F32)
        term += lax.dot_general(far, beside(*pairs[2:]), NT, preferred_element_type=F32)

        @pl.when(first)
        def _():
            acc[:, cols] = term

        @pl.when(jnp.logical_not(first))
        def _():
            acc[:, cols] += term

    @pl.when(pl.program_id(0) == 3)
    def _():
        @pl.loop(0, RANGE // 16)
        def _(i):
            gates, ups = pl.ds(i * 16, 16), pl.ds(RANGE + i * 16, 16)
            gate, up, grad = sums_ref[gates, :], sums_ref[ups, :], acc[gates, :]
            sig = jax.nn.sigmoid(gate)
            grads_ref[gates, :] = (grad * up * sig * (1.0 + gate * (1.0 - sig))).astype(BF16)
            grads_ref[ups, :] = (grad * gate * sig).astype(BF16)

        @pl.loop(0, TOKENS // 128)
        def _(i):
            part = pl.ds(pl.multiple_of(i * 128, 128), 128)
            turned_ref[part, :] = grads_ref[:, part].T


def pair_grads_kernel(pos, g_ref, a0, b0, a1, b1, out_ref):
    own, other = core_columns(pos)
    for cols, low, high in ((own, a0, a1), (other, b0, b1)):
        acts = jnp.concatenate([low[0, 0], high[0, 0]], axis=0)
        term = lax.dot_general(g_ref[...], acts, NN, preferred_element_type=F32).astype(BF16)
        out_ref[0, 0, :, cols] = term[:RANGE]
        out_ref[0, 1, :, cols] = term[RANGE:]


def down_grads_kernel(pos, h_ref, a0, b0, a1, b1, c0, d0, c1, d1, out_ref):
    own, other = core_columns(pos)
    for place, cols, low, high in ((0, own, a0, a1), (0, other, b0, b1), (1, own, c0, c1), (1, other, d0, d1)):
        acts = jnp.concatenate([low[0, 0], high[0, 0]], axis=0)
        term = lax.dot_general(h_ref[...], acts, NN, preferred_element_type=F32)
        out_ref[0, place, :, cols] = term.astype(BF16)


def token_grads_kernel(pos, g_ref, near_ref, far_ref, out_ref):
    here, far = pos[2], pl.program_id(1)
    near_w, far_w = (ref.at[0].reshape(2 * RANGE, 512)[...] for ref in (near_ref, far_ref))
    w = jnp.where(far == 0, near_w, far_w)
    term = lax.dot_general(g_ref[...], w, NN, preferred_element_type=F32).astype(BF16)
    for xl in (0, 1):
        place = turn_x(pos, far ^ pos[3], xl)
        out_ref[here, 0, place] = term[xl * 512 : (xl + 1) * 512, :256]
        out_ref[1 - here, 0, place] = term[xl * 512 : (xl + 1) * 512, 256:]


def token_grads(pos, turned, near, far_w):
    def place(z, far, pos):
        return (0, turn_y(pos, z), 0, 0, 0)

    return call(
        token_grads_kernel,
        (4, 2),
        [whole(turned.shape), by_z(2, 0), by_turned_z(2, 0)],
        [((2, 4, 4, 512, 256), BF16)],
        [pl.BlockSpec((2, 1, 4, 512, 256), place)],
        [],
        2 * FLOPS,
        (pos, turned, near, far_w),
    )[0]


def on_device(
    tokens, cotangent, gate_weight, up_weight, down_weight, gate_keep, up_keep, down_keep
):
    xl = lax.axis_index("xl")
    place_x = lax.axis_index("xh") * 2 + xl
    pos = jnp.stack(
        [place_x, lax.axis_index("y"), lax.axis_index("c"), xl, lax.axis_index("z")]
    ).astype(jnp.int32)
    barrier = lax.optimization_barrier

    def ranges(weight, tile_keep):
        kept = (weight * expand(tile_keep).astype(BF16)).T.reshape(2, RANGE, 512)
        return (
            lax.dynamic_index_in_dim(kept, xl, 0, keepdims=False),
            lax.dynamic_index_in_dim(kept, 1 - xl, 0, keepdims=False),
        )

    gate_own, gate_other = ranges(gate_weight, gate_keep)
    up_own, up_other = ranges(up_weight, up_keep)
    down_own, down_other = ranges(down_weight, down_keep)

    def over_z_sum(rows):
        return lax.psum_scatter(rows, "z", scatter_dimension=0, tiled=True)[0]

    near = lax.all_gather(jnp.stack([gate_own, up_own, down_own])[None], "z", axis=0, tiled=True)
    tokens_x = gather_four(tokens, X)
    cot_y = gather_four(cotangent, "y")
    others = jnp.stack([gate_other, up_other, down_other])
    tokens_x, cot_y, others = barrier((tokens_x, cot_y, others))
    far_here = shift(others, "xl", 2, 1)
    tokens_up, tokens_low = shift(tokens_x, "y", 4, -1), shift(tokens_x, "y", 4, 1)
    tokens_across = shift(tokens_x, "y", 4, 2)
    cot_y, far_here = barrier((cot_y, far_here))
    far = ring_gather(far_here)
    cot_own = [cot_y] + [shift(cot_y, X, 4, -d) for d in (1, 2, 3)]
    cot_own = jnp.stack(cot_own)
    tokens_own = jnp.stack([tokens_x, tokens_up, tokens_across, tokens_low])
    tokens_swap = shift(tokens_own, "c", 2, 1)
    cot_swap = shift(cot_own, "c", 2, 1)
    token_args = (tokens_own, tokens_swap, tokens_own, tokens_swap)
    cot_args = (cot_own, cot_swap, cot_own, cot_swap)

    def near_rows(s):
        return s, 0

    def far_rows(s):
        return s, 1

    rows_shape = (4, 2, RANGE, 512)
    (near_sums,) = call(
        near_sums_kernel,
        (4,),
        [by_z(2, 0)] + act_specs(near_rows, False),
        [(PAIR, F32)],
        [whole(PAIR)],
        [],
        FLOPS,
        (pos, near) + token_args,
    )
    sums, hidden = call(
        far_sums_kernel,
        (4,),
        [by_turned_z(2, 0)] + act_specs(far_rows, False) + [whole(PAIR)],
        [(PAIR, F32), (SUMS, BF16)],
        [whole(PAIR), whole(SUMS)],
        [],
        FLOPS,
        (pos, far) + token_args + (near_sums,),
    )
    (down_rows,) = call(
        down_grads_kernel,
        (4,),
        [whole(SUMS)] + act_specs(near_rows, True) + act_specs(far_rows, True),
        [(rows_shape, BF16)],
        [by_z(2, 0)],
        [],
        FLOPS,
        (pos, hidden) + cot_args + cot_args,
    )
    down_rows, sums = barrier((down_rows, sums))
    down_sum = over_z_sum(down_rows)
    grads, turned = call(
        hidden_grad_kernel,
        (4,),
        [by_z(1, 2), by_turned_z(1, 2)] + act_specs(near_rows, True) + act_specs(far_rows, True) + [whole(PAIR)],
        [(PAIR, BF16), (PAIR[::-1], BF16)],
        [whole(PAIR), whole(PAIR[::-1])],
        [pltpu.VMEM(SUMS, F32)],
        FLOPS,
        (pos, near, far) + cot_args + cot_args + (sums,),
    )

    def pair_rows(rows_of, out_spec, grads):
        return call(
            pair_grads_kernel,
            (4,),
            [whole(PAIR)] + act_specs(rows_of, False),
            [(rows_shape, BF16)],
            [out_spec],
            [],
            FLOPS,
            (pos, grads) + token_args,
        )[0]

    parts = token_grads(pos, turned, near, far)
    parts, grads = barrier((parts, grads))
    core_part = shift(parts[1], "c", 2, 1)
    far_grads = pair_rows(far_rows, by_turned_z(2, 0), grads)
    far_blocks = ring_scatter(far_grads)
    far_grads, grads = barrier((far_grads, grads))
    near_grads = pair_rows(near_rows, by_z(2, 0), grads)
    near_sum = over_z_sum(near_grads)
    of_chip = total_of((parts[0], core_part))
    y_blocks = send_four(of_chip, "y")
    down_back = shift(down_sum[1], "xl", 2, 1)
    far_row = total_of(far_blocks)
    far_back = shift(far_row, "xl", 2, 1)
    y_blocks, down_back = barrier((y_blocks, down_back))
    along_y = total_of(y_blocks)
    grad_tokens = total_of(send_four(along_y, X))
    grad_tokens, near_sum, far_back = barrier((grad_tokens, near_sum, far_back))
    gate_back, up_back = far_back[0], far_back[1]

    def own_rows(own, other, tile_keep):
        both = jnp.where(xl == 0, jnp.stack([own, other]), jnp.stack([other, own]))
        grad = both.reshape(2 * RANGE, 512).T
        return (grad.astype(F32) * expand(tile_keep).astype(F32)).astype(BF16)

    grad_down = own_rows(down_sum[0], down_back, down_keep)
    grad_gate = own_rows(near_sum[0], gate_back, gate_keep)
    grad_up = own_rows(near_sum[1], up_back, up_keep)
    return (grad_tokens, grad_gate, grad_up, grad_down)


def solution(mesh):
    fine = Mesh(mesh.devices.reshape(2, 4, 2, 4, 2), ("xl", "z", "xh", "y", "c"))
    spec = P(("xl", "z"), ("xh", "y", "c"))

    return jax.shard_map(
        on_device, mesh=fine, in_specs=(spec,) * 8, out_specs=(spec,) * 4, check_vma=False
    )
```

profile of v0, /device:TPU:0, one launch (start us, length us, event | category | flops | bytes accessed | tf_op | source)
XLA Modules:
  0.0 388.9 jit_solution(8758200259765185739)
XLA Ops:
  15.5 2.9 collective-permute-start
  20.2 3.0 collective-permute-start.3
  23.8 5.8 %collective-permute-done = bf16[512,256]{1,0:T(8,128)(2,1)S(1)} collective-permute-done((bf16[512,256]{1,0:T(8,128)(2,1)S(1)}, bf16[512,256]{1,0:T(8,128)(2,1)S(1)}, u32[]{:S(2)}, u32[]{:S(2)}) %collective-permute-start) | collective-permute-done | bytes 262176 | tf_op jit(solution)/shard_map/ppermute | solution.py:22
  33.9 3.4 collective-permute-done.5
  41.3 28.4 %collective-permute-done.6 = bf16[3,448,512]{2,1,0:T(8,128)(2,1)S(1)} collective-permute-done((bf16[3,448,512]{2,1,0:T(8,128)(2,1)S(1)}, bf16[3,448,512]{2,1,0:T(8,128)(2,1)S(1)}, u32[]{:S(2)}, u32[]{:S(2)}) %collective-permute-start.6) | collective-permute-done | bytes 1376288 | tf_op jit(solution)/shard_map/ppermute | solution.py:22
  69.7 2.7 collective-permute-start.11
  73.5 14.6 %collective-permute-done.17 = bf16[4,512,256]{2,1,0:T(8,128)(2,1)S(1)} collective-permute-done((bf16[4,512,256]{2,1,0:T(8,128)(2,1)S(1)}, bf16[4,512,256]{2,1,0:T(8,128)(2,1)S(1)}, u32[]{:S(2)}, u32[]{:S(2)}) %collective-permute-start.17) | collective-permute-done | bytes 1048608 | tf_op jit(solution)/shard_map/ppermute | solution.py:22
  90.4 5.3 %collective-permute-done.11 = bf16[4,512,256]{2,1,0:T(8,128)(2,1)S(1)} collective-permute-done((bf16[4,512,256]{2,1,0:T(8,128)(2,1)S(1)}, bf16[4,512,256]{2,1,0:T(8,128)(2,1)S(1)}, u32[]{:S(2)}, u32[]{:S(2)}) %collective-permute-start.11) | collective-permute-done | bytes 1048608 | tf_op jit(solution)/shard_map/ppermute | solution.py:22
  95.7 4.2 %collective-permute-done.12 = bf16[4,512,256]{2,1,0:T(8,128)(2,1)S(1)} collective-permute-done((bf16[4,512,256]{2,1,0:T(8,128)(2,1)S(1)}, bf16[4,512,256]{2,1,0:T(8,128)(2,1)S(1)}, u32[]{:S(2)}, u32[]{:S(2)}) %collective-permute-start.12) | collective-permute-done | bytes 1048608 | tf_op jit(solution)/shard_map/ppermute | solution.py:22
  100.0 18.7 %collective-permute-done.13 = bf16[4,512,256]{2,1,0:T(8,128)(2,1)S(1)} collective-permute-done((bf16[4,512,256]{2,1,0:T(8,128)(2,1)S(1)}, bf16[4,512,256]{2,1,0:T(8,128)(2,1)S(1)}, u32[]{:S(2)}, u32[]{:S(2)}) %collective-permute-start.13) | collective-permute-done | bytes 1048608 | tf_op jit(solution)/shard_map/ppermute | solution.py:22
  125.1 30.8 %collective-permute-done.8 = bf16[3,448,512]{2,1,0:T(8,128)(2,1)S(1)} collective-permute-done((bf16[3,448,512]{2,1,0:T(8,128)(2,1)S(1)}, bf16[3,448,512]{2,1,0:T(8,128)(2,1)S(1)}, u32[]{:S(2)}, u32[]{:S(2)}) %collective-permute-start.8) | collective-permute-done | bytes 1376288 | tf_op jit(solution)/shard_map/ppermute | solution.py:22
  157.6 3.2 collective-permute-start.10
  161.5 13.9 %collective-permute-done.9 = bf16[672,512]{1,0:T(8,128)(2,1)S(1)} collective-permute-done((bf16[672,512]{1,0:T(8,128)(2,1)}, bf16[672,512]{1,0:T(8,128)(2,1)S(1)}, u32[]{:S(2)}, u32[]{:S(2)}) %collective-permute-start.9) | collective-permute-done | bytes 688160 | tf_op jit(solution)/shard_map/ppermute | solution.py:22
  176.9 3.0 pad_maximum_fusion.w_ref.far_ref
  180.0 10.8 %shard_map.111.near_ref = f32[896,1024]{1,0:T(8,128)} custom-call(s32[5]{0:T(128)} %stack.150.pos, bf16[4,3,448,512]{3,2,1,0:T(8,128)(2,1)} %bitcast.163, bf16[4,4,512,256]{3,2,1,0:T(8,128)(2,1)} %pad_maximum_fusion.2.a0.a1, bf16[4,4,512,256]{3,2,1,0:T(8,128)(2,1)} %collective-permute-done.18.b0.b1, bf16[4,4,512,256]{3,2,1,0:T(8,128)(2,1)} %pad_maximum_fusion.2.a0.a1, ...), custom_call_target="tpu_custom_call" | custom-call | flops 3758096384 | bytes 22282260 | tf_op jit(solution)/shard_map/pallas_call | solution.py:98
  190.7 13.2 %shard_map.112 = (f32[896,1024]{1,0:T(8,128)}, bf16[448,1024]{1,0:T(8,128)(2,1)}) custom-call(s32[5]{0:T(128)} %stack.150.pos, bf16[4,3,448,512]{3,2,1,0:T(8,128)(2,1)} %pad_maximum_fusion.w_ref.far_ref, bf16[4,4,512,256]{3,2,1,0:T(8,128)(2,1)} %pad_maximum_fusion.2.a0.a1, bf16[4,4,512,256]{3,2,1,0:T(8,128)(2,1)} %collective-permute-done.18.b0.b1, ...), custom_call_target="tpu_custom_call" | custom-call | flops 3758096384 | bytes 25952276 | tf_op jit(solution)/shard_map/pallas_call | solution.py:98
  203.9 9.1 %shard_map.113 = bf16[4,2,448,512]{3,2,1,0:T(8,128)(2,1)} custom-call(s32[5]{0:T(128)} %stack.150.pos, bf16[448,1024]{1,0:T(8,128)(2,1)} %get-tuple-element.31.h_ref, bf16[4,4,512,256]{3,2,1,0:T(8,128)(2,1)} %pad_maximum_fusion.1.a0.a1.c0.c1, bf16[4,4,512,256]{3,2,1,0:T(8,128)(2,1)} %collective-permute-done.14.b0.b1.d0.d1, ...), custom_call_target="tpu_custom_call" | custom-call | flops 3758096384 | bytes 34471956 | tf_op jit(solution)/shard_map/pallas_call | solution.py:98
  213.1 14.7 %shard_map.114 = (bf16[896,1024]{1,0:T(8,128)(2,1)}, bf16[1024,896]{1,0:T(8,128)(2,1)}) custom-call(s32[5]{0:T(128)} %stack.150.pos, bf16[4,3,448,512]{3,2,1,0:T(8,128)(2,1)} %bitcast.164, bf16[4,3,448,512]{3,2,1,0:T(8,128)(2,1)} %pad_maximum_fusion.w_ref.far_ref, bf16[4,4,512,256]{3,2,1,0:T(8,128)(2,1)} %pad_maximum_fusion.1.a0.a1.c0.c1, ...), custom_call_target="tpu_custom_call" | custom-call | flops 3758096384 | bytes 48234516 | tf_op jit(solution)/shard_map/pallas_call | solution.py:98
  227.8 15.1 %shard_map.115 = bf16[2,4,4,512,256]{4,3,2,1,0:T(8,128)(2,1)} custom-call(s32[5]{0:T(128)} %stack.150.pos, bf16[1024,896]{1,0:T(8,128)(2,1)} %get-tuple-element.34.g_ref, bf16[4,3,448,512]{3,2,1,0:T(8,128)(2,1)} %bitcast.165, bf16[4,3,448,512]{3,2,1,0:T(8,128)(2,1)} %pad_maximum_fusion.w_ref.far_ref), custom_call_target="tpu_custom_call" | custom-call | flops 7516192768 | bytes 12845076 | tf_op jit(solution)/shard_map/pallas_call | solution.py:98
  242.9 4.5 %slice_bitcast_fusion = bf16[4,4,512,256]{3,2,1,0:T(8,128)(2,1)} fusion(bf16[2,4,4,512,256]{4,3,2,1,0:T(8,128)(2,1)} %shard_map.115), kind=kLoop, calls=%fused_computation.5 | loop fusion | bytes 8388608 | tf_op jit(solution)/shard_map/squeeze | solution.py:357
  247.4 8.7 %shard_map.116 = bf16[4,2,448,512]{3,2,1,0:T(8,128)(2,1)} custom-call(s32[5]{0:T(128)} %stack.150.pos, bf16[896,1024]{1,0:T(8,128)(2,1)} %get-tuple-element.43.g_ref, bf16[4,4,512,256]{3,2,1,0:T(8,128)(2,1)} %pad_maximum_fusion.2.a0.a1, bf16[4,4,512,256]{3,2,1,0:T(8,128)(2,1)} %collective-permute-done.18.b0.b1, ...), custom_call_target="tpu_custom_call" | custom-call | flops 3758096384 | bytes 18612244 | tf_op jit(solution)/shard_map/pallas_call | solution.py:98
  256.1 8.7 %shard_map.117 = bf16[4,2,448,512]{3,2,1,0:T(8,128)(2,1)} custom-call(s32[5]{0:T(128)} %stack.150.pos, bf16[896,1024]{1,0:T(8,128)(2,1)} %get-tuple-element.43.g_ref, bf16[4,4,512,256]{3,2,1,0:T(8,128)(2,1)} %pad_maximum_fusion.2.a0.a1, bf16[4,4,512,256]{3,2,1,0:T(8,128)(2,1)} %collective-permute-done.18.b0.b1, ...), custom_call_target="tpu_custom_call" | custom-call | flops 3758096384 | bytes 18612244 | tf_op jit(solution)/shard_map/pallas_call | solution.py:98
  266.4 3.5 collective-permute-start.29
  269.9 16.6 %collective-permute-done.27 = bf16[448,512]{1,0:T(8,128)(2,1)S(1)} collective-permute-done((bf16[448,512]{1,0:T(8,128)(2,1)S(1)}, bf16[448,512]{1,0:T(8,128)(2,1)S(1)}, u32[]{:S(2)}, u32[]{:S(2)}) %collective-permute-start.27) | collective-permute-done | bytes 458784 | tf_op jit(solution)/shard_map/ppermute | solution.py:22
  292.5 3.7 collective-permute-start.30
  296.2 4.7 %fusion = bf16[4,4,512,256]{3,2,1,0:T(8,128)(2,1)S(1)} fusion(bf16[4,4,512,256]{3,2,1,0:T(8,128)(2,1)} %collective-permute-done.19, bf16[2,4,4,512,256]{4,3,2,1,0:T(8,128)(2,1)} %shard_map.115), kind=kLoop, calls=%fused_computation.1 | loop fusion | flops 8388608 | bytes 12582912 | tf_op jit(solution)/shard_map/convert_element_type | solution.py:58
  308.2 22.0 %collective-permute-done.28 = bf16[2,448,512]{2,1,0:T(8,128)(2,1)S(1)} collective-permute-done((bf16[2,448,512]{2,1,0:T(8,128)(2,1)}, bf16[2,448,512]{2,1,0:T(8,128)(2,1)S(1)}, u32[]{:S(2)}, u32[]{:S(2)}) %collective-permute-start.28) | collective-permute-done | bytes 917536 | tf_op jit(solution)/shard_map/ppermute | solution.py:22
  332.0 2.7 fusion.5
  335.3 15.2 %collective-permute-done.20 = bf16[4,512,256]{2,1,0:T(8,128)(2,1)S(1)} collective-permute-done((bf16[4,512,256]{2,1,0:T(8,128)(2,1)}, bf16[4,512,256]{2,1,0:T(8,128)(2,1)S(1)}, u32[]{:S(2)}, u32[]{:S(2)}) %collective-permute-start.20) | collective-permute-done | bytes 1048608 | tf_op jit(solution)/shard_map/ppermute | solution.py:22
  356.2 2.7 collective-permute-start.26
  362.2 6.0 %collective-permute-done.24 = bf16[512,256]{1,0:T(8,128)(2,1)} collective-permute-done((bf16[512,256]{1,0:T(8,128)(2,1)}, bf16[512,256]{1,0:T(8,128)(2,1)}, u32[]{:S(2)}, u32[]{:S(2)}) %collective-permute-start.24) | collective-permute-done | bytes 262176 | tf_op jit(solution)/shard_map/ppermute | solution.py:22
  368.2 5.2 %collective-permute-done.25 = bf16[512,256]{1,0:T(8,128)(2,1)} collective-permute-done((bf16[512,256]{1,0:T(8,128)(2,1)}, bf16[512,256]{1,0:T(8,128)(2,1)}, u32[]{:S(2)}, u32[]{:S(2)}) %collective-permute-start.25) | collective-permute-done | bytes 262176 | tf_op jit(solution)/shard_map/ppermute | solution.py:22
  (119 shorter events, 67.5 us)
Async XLA Ops:
  7.2 172.8 %all-gather.3.cloned.1.call-start = ((), (), s32[]{:S(2)}) async-start(), calls=%async_computation.4 | async-start | bytes 6881280 | tf_op jit(solution)/shard_map/all_gather | solution.py:275
  15.5 290.7 %reduce-scatter.3.cloned.1.call-start = ((), (), s32[]{:S(2)}) async-start(), calls=%async_computation.2 | async-start | bytes 4587520 | tf_op jit(solution)/shard_map/reduce_scatter | solution.py:273
  15.5 14.1 %collective-permute-start = (bf16[512,256]{1,0:T(8,128)(2,1)S(1)}, bf16[512,256]{1,0:T(8,128)(2,1)S(1)}, u32[]{:S(2)}, u32[]{:S(2)}) collective-permute-start(bf16[512,256]{1,0:T(8,128)(2,1)S(1)} %copy-done.4), channel_id=1, source_target_pairs={{0,72},{64,0},{8,64},{72,8},{1,73},{65,1},{9,65},{73,9},{2,74},{66... | collective-permute-start | bytes 786440 | tf_op jit(solution)/shard_map/ppermute | solution.py:22
  19.3 14.1 %collective-permute-start.2 = (bf16[512,256]{1,0:T(8,128)(2,1)S(1)}, bf16[512,256]{1,0:T(8,128)(2,1)S(1)}, u32[]{:S(2)}, u32[]{:S(2)}) collective-permute-start(bf16[512,256]{1,0:T(8,128)(2,1)S(1)} %copy-done.4), channel_id=1, source_target_pairs={{0,64},{64,8},{8,72},{72,0},{1,65},{65,9},{9,73},{73,1},{2,66},{66... | collective-permute-start | bytes 786440 | tf_op jit(solution)/shard_map/ppermute | solution.py:22
  20.2 13.4 %collective-permute-start.3 = (bf16[512,256]{1,0:T(8,128)(2,1)S(1)}, bf16[512,256]{1,0:T(8,128)(2,1)S(1)}, u32[]{:S(2)}, u32[]{:S(2)}) collective-permute-start(bf16[512,256]{1,0:T(8,128)(2,1)S(1)} %copy-done.5), channel_id=1, source_target_pairs={{0,6},{2,0},{4,2},{6,4},{1,7},{3,1},{5,3},{7,5},{8,14},{10,8},{12,... | collective-permute-start | bytes 786440 | tf_op jit(solution)/shard_map/ppermute | solution.py:22
  37.4 32.3 %collective-permute-start.6 = (bf16[3,448,512]{2,1,0:T(8,128)(2,1)S(1)}, bf16[3,448,512]{2,1,0:T(8,128)(2,1)S(1)}, u32[]{:S(2)}, u32[]{:S(2)}) collective-permute-start(bf16[3,448,512]{2,1,0:T(8,128)(2,1)S(1)} %pad_maximum_fusion.4), channel_id=1, source_target_pairs={{0,64},{64,0},{1,65},{65,1},{2,66},{66,2},{3,67},{67,3},{4,68},{68... | collective-permute-start | bytes 4128776 | tf_op jit(solution)/shard_map/ppermute | solution.py:22
  39.2 34.3 %collective-permute-start.15 = (bf16[4,512,256]{2,1,0:T(8,128)(2,1)S(1)}, bf16[4,512,256]{2,1,0:T(8,128)(2,1)S(1)}, u32[]{:S(2)}, u32[]{:S(2)}) collective-permute-start(bf16[4,512,256]{2,1,0:T(8,128)(2,1)S(1)} %pad_maximum_fusion.6), channel_id=1, source_target_pairs={{0,6},{2,0},{4,2},{6,4},{1,7},{3,1},{5,3},{7,5},{8,14},{10,8},{12,... | collective-permute-start | bytes 3145736 | tf_op jit(solution)/shard_map/ppermute | solution.py:22
  39.8 33.7 %collective-permute-start.16 = (bf16[4,512,256]{2,1,0:T(8,128)(2,1)S(1)}, bf16[4,512,256]{2,1,0:T(8,128)(2,1)S(1)}, u32[]{:S(2)}, u32[]{:S(2)}) collective-permute-start(bf16[4,512,256]{2,1,0:T(8,128)(2,1)S(1)} %pad_maximum_fusion.6), channel_id=1, source_target_pairs={{0,4},{2,6},{4,0},{6,2},{1,5},{3,7},{5,1},{7,3},{8,12},{10,14},{12... | collective-permute-start | bytes 3145736 | tf_op jit(solution)/shard_map/ppermute | solution.py:22
  40.5 47.7 %collective-permute-start.17 = (bf16[4,512,256]{2,1,0:T(8,128)(2,1)S(1)}, bf16[4,512,256]{2,1,0:T(8,128)(2,1)S(1)}, u32[]{:S(2)}, u32[]{:S(2)}) collective-permute-start(bf16[4,512,256]{2,1,0:T(8,128)(2,1)S(1)} %pad_maximum_fusion.6), channel_id=1, source_target_pairs={{0,2},{2,4},{4,6},{6,0},{1,3},{3,5},{5,7},{7,1},{8,10},{10,12},{12... | collective-permute-start | bytes 3145736 | tf_op jit(solution)/shard_map/ppermute | solution.py:22
  69.7 26.0 %collective-permute-start.11 = (bf16[4,512,256]{2,1,0:T(8,128)(2,1)S(1)}, bf16[4,512,256]{2,1,0:T(8,128)(2,1)S(1)}, u32[]{:S(2)}, u32[]{:S(2)}) collective-permute-start(bf16[4,512,256]{2,1,0:T(8,128)(2,1)S(1)} %pad_maximum_fusion.7), channel_id=1, source_target_pairs={{0,72},{64,0},{8,64},{72,8},{1,73},{65,1},{9,65},{73,9},{2,74},{66... | collective-permute-start | bytes 3145736 | tf_op jit(solution)/shard_map/ppermute | solution.py:22
  72.4 27.6 %collective-permute-start.12 = (bf16[4,512,256]{2,1,0:T(8,128)(2,1)S(1)}, bf16[4,512,256]{2,1,0:T(8,128)(2,1)S(1)}, u32[]{:S(2)}, u32[]{:S(2)}) collective-permute-start(bf16[4,512,256]{2,1,0:T(8,128)(2,1)S(1)} %pad_maximum_fusion.7), channel_id=1, source_target_pairs={{0,8},{64,72},{8,0},{72,64},{1,9},{65,73},{9,1},{73,65},{2,10},{66... | collective-permute-start | bytes 3145736 | tf_op jit(solution)/shard_map/ppermute | solution.py:22
  73.5 45.2 %collective-permute-start.13 = (bf16[4,512,256]{2,1,0:T(8,128)(2,1)S(1)}, bf16[4,512,256]{2,1,0:T(8,128)(2,1)S(1)}, u32[]{:S(2)}, u32[]{:S(2)}) collective-permute-start(bf16[4,512,256]{2,1,0:T(8,128)(2,1)S(1)} %pad_maximum_fusion.7), channel_id=1, source_target_pairs={{0,64},{64,8},{8,72},{72,0},{1,65},{65,9},{9,73},{73,1},{2,66},{66... | collective-permute-start | bytes 3145736 | tf_op jit(solution)/shard_map/ppermute | solution.py:22
  90.4 89.6 %collective-permute-start.18 = (bf16[4,4,512,256]{3,2,1,0:T(8,128)(2,1)}, bf16[4,4,512,256]{3,2,1,0:T(8,128)(2,1)}, u32[]{:S(2)}, u32[]{:S(2)}) collective-permute-start(bf16[4,4,512,256]{3,2,1,0:T(8,128)(2,1)} %pad_maximum_fusion.2.a0.a1), channel_id=1, source_target_pairs={{0,1},{1,0},{2,3},{3,2},{4,5},{5,4},{6,7},{7,6},{8,9},{9,8},{10,11... | collective-permute-start | bytes 12582920 | tf_op jit(solution)/shard_map/ppermute | solution.py:22
  121.0 83.0 %collective-permute-start.14 = (bf16[4,4,512,256]{3,2,1,0:T(8,128)(2,1)}, bf16[4,4,512,256]{3,2,1,0:T(8,128)(2,1)}, u32[]{:S(2)}, u32[]{:S(2)}) collective-permute-start(bf16[4,4,512,256]{3,2,1,0:T(8,128)(2,1)} %pad_maximum_fusion.1.a0.a1.c0.c1), channel_id=1, source_target_pairs={{0,1},{1,0},{2,3},{3,2},{4,5},{5,4},{6,7},{7,6},{8,9},{9,8},{10,11... | collective-permute-start | bytes 12582920 | tf_op jit(solution)/shard_map/ppermute | solution.py:22
  121.0 34.9 %collective-permute-start.8 = (bf16[3,448,512]{2,1,0:T(8,128)(2,1)S(1)}, bf16[3,448,512]{2,1,0:T(8,128)(2,1)S(1)}, u32[]{:S(2)}, u32[]{:S(2)}) collective-permute-start(bf16[3,448,512]{2,1,0:T(8,128)(2,1)S(1)} %collective-permute-done.6), channel_id=1, source_target_pairs={{0,16},{16,32},{32,48},{48,0},{1,17},{17,33},{33,49},{49,1},{2,18}... | collective-permute-start | bytes 4128776 | tf_op jit(solution)/shard_map/ppermute | solution.py:22
  122.7 34.1 %collective-permute-start.7 = (bf16[3,448,512]{2,1,0:T(8,128)(2,1)S(1)}, bf16[3,448,512]{2,1,0:T(8,128)(2,1)S(1)}, u32[]{:S(2)}, u32[]{:S(2)}) collective-permute-start(bf16[3,448,512]{2,1,0:T(8,128)(2,1)S(1)} %collective-permute-done.6), channel_id=1, source_target_pairs={{0,48},{16,0},{32,16},{48,32},{1,49},{17,1},{33,17},{49,33},{2,50}... | collective-permute-start | bytes 4128776 | tf_op jit(solution)/shard_map/ppermute | solution.py:22
  156.7 18.7 %collective-permute-start.9 = (bf16[672,512]{1,0:T(8,128)(2,1)}, bf16[672,512]{1,0:T(8,128)(2,1)S(1)}, u32[]{:S(2)}, u32[]{:S(2)}) collective-permute-start(bf16[672,512]{1,0:T(8,128)(2,1)} %slice_bitcast_fusion.7), channel_id=1, source_target_pairs={{0,16},{16,32},{32,48},{48,0},{1,17},{17,33},{33,49},{49,1},{2,18}... | collective-permute-start | bytes 2064392 | tf_op jit(solution)/shard_map/ppermute | solution.py:22
  157.6 18.0 %collective-permute-start.10 = (bf16[672,512]{1,0:T(8,128)(2,1)}, bf16[672,512]{1,0:T(8,128)(2,1)}, u32[]{:S(2)}, u32[]{:S(2)}) collective-permute-start(bf16[672,512]{1,0:T(8,128)(2,1)} %slice_bitcast_fusion.6), channel_id=1, source_target_pairs={{0,48},{16,0},{32,16},{48,32},{1,49},{17,1},{33,17},{49,33},{2,50}... | collective-permute-start | bytes 2064392 | tf_op jit(solution)/shard_map/ppermute | solution.py:22
  213.1 162.5 %reduce-scatter.5.cloned.1.call-start = ((), (), s32[]{:S(2)}) async-start(), calls=%async_computation.3 | async-start | bytes 4587520 | tf_op jit(solution)/shard_map/reduce_scatter | solution.py:273
  247.4 48.7 %collective-permute-start.19 = (bf16[4,4,512,256]{3,2,1,0:T(8,128)(2,1)}, bf16[4,4,512,256]{3,2,1,0:T(8,128)(2,1)}, u32[]{:S(2)}, u32[]{:S(2)}) collective-permute-start(bf16[4,4,512,256]{3,2,1,0:T(8,128)(2,1)} %slice_bitcast_fusion), channel_id=1, source_target_pairs={{0,1},{1,0},{2,3},{3,2},{4,5},{5,4},{6,7},{7,6},{8,9},{9,8},{10,11... | collective-permute-start | bytes 12582920 | tf_op jit(solution)/shard_map/ppermute | solution.py:22
  266.3 20.2 %collective-permute-start.27 = (bf16[448,512]{1,0:T(8,128)(2,1)S(1)}, bf16[448,512]{1,0:T(8,128)(2,1)S(1)}, u32[]{:S(2)}, u32[]{:S(2)}) collective-permute-start(bf16[448,512]{1,0:T(8,128)(2,1)S(1)} %get-tuple-element.62), channel_id=1, source_target_pairs={{0,16},{16,32},{32,48},{48,0},{1,17},{17,33},{33,49},{49,1},{2,18}... | collective-permute-start | bytes 1376264 | tf_op jit(solution)/shard_map/ppermute | solution.py:22
  266.4 22.6 %collective-permute-start.29 = (bf16[448,512]{1,0:T(8,128)(2,1)S(1)}, bf16[448,512]{1,0:T(8,128)(2,1)S(1)}, u32[]{:S(2)}, u32[]{:S(2)}) collective-permute-start(bf16[448,512]{1,0:T(8,128)(2,1)S(1)} %get-tuple-element.63), channel_id=1, source_target_pairs={{0,48},{16,0},{32,16},{48,32},{1,49},{17,1},{33,17},{49,33},{2,50}... | collective-permute-start | bytes 1376264 | tf_op jit(solution)/shard_map/ppermute | solution.py:22
  291.5 38.7 %collective-permute-start.28 = (bf16[2,448,512]{2,1,0:T(8,128)(2,1)}, bf16[2,448,512]{2,1,0:T(8,128)(2,1)S(1)}, u32[]{:S(2)}, u32[]{:S(2)}) collective-permute-start(bf16[2,448,512]{2,1,0:T(8,128)(2,1)} %pad_maximum_fusion.8), channel_id=1, source_target_pairs={{0,16},{16,32},{32,48},{48,0},{1,17},{17,33},{33,49},{49,1},{2,18}... | collective-permute-start | bytes 2752520 | tf_op jit(solution)/shard_map/ppermute | solution.py:22
  292.5 39.5 %collective-permute-start.30 = (bf16[2,448,512]{2,1,0:T(8,128)(2,1)}, bf16[2,448,512]{2,1,0:T(8,128)(2,1)}, u32[]{:S(2)}, u32[]{:S(2)}) collective-permute-start(bf16[2,448,512]{2,1,0:T(8,128)(2,1)} %pad_maximum_fusion.9), channel_id=1, source_target_pairs={{0,48},{16,0},{32,16},{48,32},{1,49},{17,1},{33,17},{49,33},{2,50}... | collective-permute-start | bytes 2752520 | tf_op jit(solution)/shard_map/ppermute | solution.py:22
  302.7 47.8 %collective-permute-start.20 = (bf16[4,512,256]{2,1,0:T(8,128)(2,1)}, bf16[4,512,256]{2,1,0:T(8,128)(2,1)S(1)}, u32[]{:S(2)}, u32[]{:S(2)}) collective-permute-start(bf16[4,512,256]{2,1,0:T(8,128)(2,1)} %get-tuple-element.58), channel_id=1, source_target_pairs={{0,2},{2,4},{4,6},{6,0},{1,3},{3,5},{5,7},{7,1},{8,10},{10,12},{12... | collective-permute-start | bytes 3145736 | tf_op jit(solution)/shard_map/ppermute | solution.py:22
  302.7 47.8 %collective-permute-start.21 = (bf16[4,512,256]{2,1,0:T(8,128)(2,1)}, bf16[4,512,256]{2,1,0:T(8,128)(2,1)}, u32[]{:S(2)}, u32[]{:S(2)}) collective-permute-start(bf16[4,512,256]{2,1,0:T(8,128)(2,1)} %get-tuple-element.57), channel_id=1, source_target_pairs={{0,4},{2,6},{4,0},{6,2},{1,5},{3,7},{5,1},{7,3},{8,12},{10,14},{12... | collective-permute-start | bytes 3145736 | tf_op jit(solution)/shard_map/ppermute | solution.py:22
  304.2 47.1 %collective-permute-start.22 = (bf16[4,512,256]{2,1,0:T(8,128)(2,1)}, bf16[4,512,256]{2,1,0:T(8,128)(2,1)}, u32[]{:S(2)}, u32[]{:S(2)}) collective-permute-start(bf16[4,512,256]{2,1,0:T(8,128)(2,1)} %get-tuple-element.56), channel_id=1, source_target_pairs={{0,6},{2,0},{4,2},{6,4},{1,7},{3,1},{5,3},{7,5},{8,14},{10,8},{12,... | collective-permute-start | bytes 3145736 | tf_op jit(solution)/shard_map/ppermute | solution.py:22
  330.2 21.0 %collective-permute-start.23 = (bf16[448,512]{1,0:T(8,128)(2,1)}, bf16[448,512]{1,0:T(8,128)(2,1)}, u32[]{:S(2)}, u32[]{:S(2)}) collective-permute-start(bf16[448,512]{1,0:T(8,128)(2,1)} %get-tuple-element.70), channel_id=1, source_target_pairs={{0,64},{64,0},{1,65},{65,1},{2,66},{66,2},{3,67},{67,3},{4,68},{68... | collective-permute-start | bytes 1376264 | tf_op jit(solution)/shard_map/ppermute | solution.py:22
  334.7 40.8 %collective-permute-start.31 = (bf16[2,448,512]{2,1,0:T(8,128)(2,1)}, bf16[2,448,512]{2,1,0:T(8,128)(2,1)}, u32[]{:S(2)}, u32[]{:S(2)}) collective-permute-start(bf16[2,448,512]{2,1,0:T(8,128)(2,1)} %fusion.5), channel_id=1, source_target_pairs={{0,64},{64,0},{1,65},{65,1},{2,66},{66,2},{3,67},{67,3},{4,68},{68... | collective-permute-start | bytes 2752520 | tf_op jit(solution)/shard_map/ppermute | solution.py:22
  354.8 13.4 %collective-permute-start.24 = (bf16[512,256]{1,0:T(8,128)(2,1)}, bf16[512,256]{1,0:T(8,128)(2,1)}, u32[]{:S(2)}, u32[]{:S(2)}) collective-permute-start(bf16[512,256]{1,0:T(8,128)(2,1)} %get-tuple-element.66), channel_id=1, source_target_pairs={{0,64},{64,8},{8,72},{72,0},{1,65},{65,9},{9,73},{73,1},{2,66},{66... | collective-permute-start | bytes 786440 | tf_op jit(solution)/shard_map/ppermute | solution.py:22
  356.2 17.3 %collective-permute-start.25 = (bf16[512,256]{1,0:T(8,128)(2,1)}, bf16[512,256]{1,0:T(8,128)(2,1)}, u32[]{:S(2)}, u32[]{:S(2)}) collective-permute-start(bf16[512,256]{1,0:T(8,128)(2,1)} %get-tuple-element.68), channel_id=1, source_target_pairs={{0,8},{64,72},{8,0},{72,64},{1,9},{65,73},{9,1},{73,65},{2,10},{66... | collective-permute-start | bytes 786440 | tf_op jit(solution)/shard_map/ppermute | solution.py:22
  356.2 17.5 %collective-permute-start.26 = (bf16[512,256]{1,0:T(8,128)(2,1)}, bf16[512,256]{1,0:T(8,128)(2,1)}, u32[]{:S(2)}, u32[]{:S(2)}) collective-permute-start(bf16[512,256]{1,0:T(8,128)(2,1)} %get-tuple-element.67), channel_id=1, source_target_pairs={{0,72},{64,0},{8,64},{72,8},{1,73},{65,1},{9,65},{73,9},{2,74},{66... | collective-permute-start | bytes 786440 | tf_op jit(solution)/shard_map/ppermute | solution.py:22
  (10 other events, 115.1 us)
Sparse Core Ops, SparseCore 0:
  15.6 61.7 all-gather.2
  213.2 41.9 reduce-scatter.2
  264.9 61.6 reduce-scatter.4
where the time goes:
time: 390 us; the launch traced here: 389 us
  waiting for transfers between devices  196 us (50%)
  Pallas kernels  80.2 us (21%)
  starting transfers between devices  41.9 us (11%)
  other arithmetic  30.5 us (8%)
  local copies, waits for them, and re-layouts  25.7 us (7%)
  between operations  14.1 us (4%)
    ppermute x32, waiting for transfers between devices, shift(): lax.ppermute(value, axis, [(name(i), name((i + step) % size)) for i in ra...  196 us
    pallas_call x7, Pallas kernels, call(): pl.pallas_call(kernel, out_shape=[jax.ShapeDtypeStruct(shape, kind) for s...  80.2 us
    ppermute x32, starting transfers between devices, shift(): lax.ppermute(value, axis, [(name(i), name((i + step) % size)) for i in ra...  41.8 us
    convert_element_type x4, other arithmetic, total_of(): return sum((b.astype(F32) for b in blocks)).astype(BF16)  11.8 us
  transfers between devices with their start and end apart: 35, of which 20 were waited for; matrix products, arithmetic and copies ran while one was open for 11% of the time, Pallas kernels for 18%

commit v1 on v0

--- a/solution.py
+++ b/solution.py
@@ -43,15 +43,6 @@
         [shift(left.reshape(cut)[0], "z", 4, 1), shift(right.reshape(cut)[1], "z", 4, -1)]
     )
     return jnp.stack([block, right, across.reshape(block.shape), left])
-
-
-def ring_scatter(pieces):
-    own, right, across, left = (pieces[d] for d in range(4))
-    low, high = shift(across[0], "z", 4, 1), shift(across[1], "z", 4, -1)
-    right_0, right_1, left_0, left_1 = right[0], right[1], left[0], left[1]
-    right_0, left_1 = total_of((right_0, low)), total_of((left_1, high))
-    to_right, to_left = jnp.stack([right_0, right_1]), jnp.stack([left_0, left_1])
-    return [own, shift(to_right, "z", 4, 1), shift(to_left, "z", 4, -1)]
 
 
 def total_of(blocks):
@@ -239,7 +230,7 @@
     return call(
         token_grads_kernel,
         (4, 2),
-        [whole(turned.shape), by_z(2, 0), by_turned_z(2, 0)],
+        [whole(turned.shape), by_z(2, 0), by_z(2, 0)],
         [((2, 4, 4, 512, 256), BF16)],
         [pl.BlockSpec((2, 1, 4, 512, 256), place)],
         [],
@@ -257,6 +248,7 @@
         [place_x, lax.axis_index("y"), lax.axis_index("c"), xl, lax.axis_index("z")]
     ).astype(jnp.int32)
     barrier = lax.optimization_barrier
+    one = (pos[4] < 4).astype(BF16)
 
     def ranges(weight, tile_keep):
         kept = (weight * expand(tile_keep).astype(BF16)).T.reshape(2, RANGE, 512)
@@ -272,16 +264,23 @@
     def over_z_sum(rows):
         return lax.psum_scatter(rows, "z", scatter_dimension=0, tiled=True)[0]
 
-    near = lax.all_gather(jnp.stack([gate_own, up_own, down_own])[None], "z", axis=0, tiled=True)
+    def over_z(rows):
+        return lax.all_gather(rows[None], "z", axis=0, tiled=True)
+
+    near = over_z(jnp.stack([gate_own, up_own]))
     tokens_x = gather_four(tokens, X)
     cot_y = gather_four(cotangent, "y")
-    others = jnp.stack([gate_other, up_other, down_other])
-    tokens_x, cot_y, others = barrier((tokens_x, cot_y, others))
-    far_here = shift(others, "xl", 2, 1)
+    tokens_x, cot_y, gate_other, up_other, down_other = barrier(
+        (tokens_x, cot_y, gate_other, up_other, down_other)
+    )
+    gate_far, up_far = shift(gate_other, "xl", 2, 1), shift(up_other, "xl", 2, 1)
+    down_far = shift(down_other, "xl", 2, 1)
+    far_here = jnp.stack([gate_far, up_far])
+    far = over_z(far_here)
     tokens_up, tokens_low = shift(tokens_x, "y", 4, -1), shift(tokens_x, "y", 4, 1)
     tokens_across = shift(tokens_x, "y", 4, 2)
-    cot_y, far_here = barrier((cot_y, far_here))
-    far = ring_gather(far_here)
+    cot_y, _ = barrier((cot_y, far_here))
+    down = ring_gather(jnp.stack([down_own, down_far]))
     cot_own = [cot_y] + [shift(cot_y, X, 4, -d) for d in (1, 2, 3)]
     cot_own = jnp.stack(cot_own)
     tokens_own = jnp.stack([tokens_x, tokens_up, tokens_across, tokens_low])
@@ -310,7 +309,7 @@
     sums, hidden = call(
         far_sums_kernel,
         (4,),
-        [by_turned_z(2, 0)] + act_specs(far_rows, False) + [whole(PAIR)],
+        [by_z(2, 0)] + act_specs(far_rows, False) + [whole(PAIR)],
         [(PAIR, F32), (SUMS, BF16)],
         [whole(PAIR), whole(SUMS)],
         [],
@@ -332,12 +331,12 @@
     grads, turned = call(
         hidden_grad_kernel,
         (4,),
-        [by_z(1, 2), by_turned_z(1, 2)] + act_specs(near_rows, True) + act_specs(far_rows, True) + [whole(PAIR)],
+        [by_turned_z(1, 0), by_turned_z(1, 1)] + act_specs(near_rows, True) + act_specs(far_rows, True) + [whole(PAIR)],
         [(PAIR, BF16), (PAIR[::-1], BF16)],
         [whole(PAIR), whole(PAIR[::-1])],
         [pltpu.VMEM(SUMS, F32)],
         FLOPS,
-        (pos, near, far) + cot_args + cot_args + (sums,),
+        (pos, down, down) + cot_args + cot_args + (sums,),
     )
 
     def pair_rows(rows_of, out_spec, grads):
@@ -355,15 +354,15 @@
     parts = token_grads(pos, turned, near, far)
     parts, grads = barrier((parts, grads))
     core_part = shift(parts[1], "c", 2, 1)
-    far_grads = pair_rows(far_rows, by_turned_z(2, 0), grads)
-    far_blocks = ring_scatter(far_grads)
+    far_grads = pair_rows(far_rows, by_z(2, 0), grads)
+    far_sum = over_z_sum(far_grads)
     far_grads, grads = barrier((far_grads, grads))
     near_grads = pair_rows(near_rows, by_z(2, 0), grads)
     near_sum = over_z_sum(near_grads)
     of_chip = total_of((parts[0], core_part))
     y_blocks = send_four(of_chip, "y")
     down_back = shift(down_sum[1], "xl", 2, 1)
-    far_row = total_of(far_blocks)
+    far_row = far_sum * one
     far_back = shift(far_row, "xl", 2, 1)
     y_blocks, down_back = barrier((y_blocks, down_back))
     along_y = total_of(y_blocks)

time: 390 us -> 363 us (0.931)
  waiting for transfers between devices: 196 us -> 178 us
    ppermute x32 -> x30, waiting for transfers between devices: 196 us -> 164 us  [shift(): lax.ppermute(value, axis, [(name(i), name((i + step) % size)) for i in ra...]
    reduce_scatter x2 -> x3, waiting for transfers between devices: 0.01 us -> 13.8 us  [over_z_sum(): return lax.psum_scatter(rows, 'z', scatter_dimension=0, tiled=True)[0]]
    another operation x6 -> x2, other arithmetic: 6.09 us -> 2.01 us  [the longest x1 1 us: on_device(): far_here = jnp.stack([gate_far, up_far])]
    convert_element_type x4 -> x3, other arithmetic: 11.8 us -> 9.13 us  [total_of(): return sum((b.astype(F32) for b in blocks)).astype(BF16)]
    ppermute x32 -> x30, starting transfers between devices: 41.8 us -> 40 us  [shift(): lax.ppermute(value, axis, [(name(i), name((i + step) % size)) for i in ra...]
  transfers between devices with their start and end apart: 35 -> 35, of which waited for: 20 -> 18; matrix products, arithmetic and copies ran while one was open for 11% -> 10% of each run, Pallas kernels for 18% -> 19%
where the time goes in v1:
time: 363 us; the launch traced here: 362 us
  waiting for transfers between devices  178 us (49%)
  Pallas kernels  79.5 us (22%)
  starting transfers between devices  40.2 us (11%)
  other arithmetic  27.7 us (8%)
  local copies, waits for them, and re-layouts  22.3 us (6%)
  between operations  14.1 us (4%)
    ppermute x30, waiting for transfers between devices, shift(): lax.ppermute(value, axis, [(name(i), name((i + step) % size)) for i in ra...  164 us
    pallas_call x7, Pallas kernels, call(): pl.pallas_call(kernel, out_shape=[jax.ShapeDtypeStruct(shape, kind) for s...  79.5 us
    ppermute x30, starting transfers between devices, shift(): lax.ppermute(value, axis, [(name(i), name((i + step) % size)) for i in ra...  40 us
    reduce_scatter x3, waiting for transfers between devices, over_z_sum(): return lax.psum_scatter(rows, 'z', scatter_dimension=0, tiled=True)[0]  13.8 us
    convert_element_type x3, other arithmetic, total_of(): return sum((b.astype(F32) for b in blocks)).astype(BF16)  9.13 us
    unnamed x20, local copies, waits for them, and re-layouts  7.3 us
  transfers between devices with their start and end apart: 35, of which 18 were waited for; matrix products, arithmetic and copies ran while one was open for 10% of the time, Pallas kernels for 19%

profile of v1, /device:TPU:0, one launch (start us, length us, event | category | flops | bytes accessed | tf_op | source)
XLA Modules:
  0.0 361.9 jit_solution(12871630975204847236)
XLA Ops:
  20.0 3.0 collective-permute-start.3
  26.1 4.9 %collective-permute-done.1 = bf16[512,256]{1,0:T(8,128)(2,1)} collective-permute-done((bf16[512,256]{1,0:T(8,128)(2,1)S(1)}, bf16[512,256]{1,0:T(8,128)(2,1)}, u32[]{:S(2)}, u32[]{:S(2)}) %collective-permute-start.1) | collective-permute-done | bytes 262176 | tf_op jit(solution)/shard_map/ppermute | solution.py:22
  34.1 3.2 collective-permute-done.5
  42.7 9.9 %collective-permute-done.11 = bf16[448,512]{1,0:T(8,128)(2,1)S(1)} collective-permute-done((bf16[448,512]{1,0:T(8,128)(2,1)S(1)}, bf16[448,512]{1,0:T(8,128)(2,1)S(1)}, u32[]{:S(2)}, u32[]{:S(2)}) %collective-permute-start.11) | collective-permute-done | bytes 458784 | tf_op jit(solution)/shard_map/ppermute | solution.py:22
  52.6 8.3 %collective-permute-done.12 = bf16[448,512]{1,0:T(8,128)(2,1)S(1)} collective-permute-done((bf16[448,512]{1,0:T(8,128)(2,1)S(1)}, bf16[448,512]{1,0:T(8,128)(2,1)S(1)}, u32[]{:S(2)}, u32[]{:S(2)}) %collective-permute-start.12) | collective-permute-done | bytes 458784 | tf_op jit(solution)/shard_map/ppermute | solution.py:22
  65.4 3.6 collective-permute-done.18
  69.0 20.4 %collective-permute-done.19 = bf16[4,512,256]{2,1,0:T(8,128)(2,1)} collective-permute-done((bf16[4,512,256]{2,1,0:T(8,128)(2,1)S(1)}, bf16[4,512,256]{2,1,0:T(8,128)(2,1)}, u32[]{:S(2)}, u32[]{:S(2)}) %collective-permute-start.19) | collective-permute-done | bytes 1048608 | tf_op jit(solution)/shard_map/ppermute | solution.py:22
  89.3 3.7 %pad_maximum_fusion.1.a0.a1 = bf16[4,4,512,256]{3,2,1,0:T(8,128)(2,1)} fusion(bf16[1,4,512,256]{3,2,1,0:T(8,128)(2,1)} %bitcast.42, bf16[1,4,512,256]{3,2,1,0:T(8,128)(2,1)} %bitcast.41, bf16[1,4,512,256]{3,2,1,0:T(8,128)(2,1)} %bitcast.40, bf16[1,4,512,256]{3,2,1,0:T(8,128)(2,1)S(1)} %bitcast.152), kind=kLoop, calls=%fused_computation.3 | loop fusion | flops 6291456 | bytes 8388608 | tf_op jit(solution)/shard_map/stack | solution.py:286
  93.0 16.9 %collective-permute-done.15 = bf16[4,512,256]{2,1,0:T(8,128)(2,1)S(1)} collective-permute-done((bf16[4,512,256]{2,1,0:T(8,128)(2,1)S(1)}, bf16[4,512,256]{2,1,0:T(8,128)(2,1)S(1)}, u32[]{:S(2)}, u32[]{:S(2)}) %collective-permute-start.15) | collective-permute-done | bytes 1048608 | tf_op jit(solution)/shard_map/ppermute | solution.py:22
  110.0 2.3 pad_maximum_fusion.a0.a1.c0.c1
  112.9 10.7 %shard_map.111.near_ref = f32[896,1024]{1,0:T(8,128)} custom-call(s32[5]{0:T(128)} %stack.150.pos, bf16[4,2,448,512]{3,2,1,0:T(8,128)(2,1)} %bitcast.157, bf16[4,4,512,256]{3,2,1,0:T(8,128)(2,1)} %pad_maximum_fusion.1.a0.a1, bf16[4,4,512,256]{3,2,1,0:T(8,128)(2,1)} %collective-permute-done.20.b0.b1, bf16[4,4,512,256]{3,2,1,0:T(8,128)(2,1)} %pad_maximum_fusion.1.a0.a1, ...), custom_call_target="tpu_custom_call" | custom-call | flops 3758096384 | bytes 20447252 | tf_op jit(solution)/shard_map/pallas_call | solution.py:89
  123.7 13.2 %shard_map.112 = (f32[896,1024]{1,0:T(8,128)}, bf16[448,1024]{1,0:T(8,128)(2,1)}) custom-call(s32[5]{0:T(128)} %stack.150.pos, bf16[4,2,448,512]{3,2,1,0:T(8,128)(2,1)} %bitcast.159, bf16[4,4,512,256]{3,2,1,0:T(8,128)(2,1)} %pad_maximum_fusion.1.a0.a1, bf16[4,4,512,256]{3,2,1,0:T(8,128)(2,1)} %collective-permute-done.20.b0.b1, ...), custom_call_target="tpu_custom_call" | custom-call | flops 3758096384 | bytes 24117268 | tf_op jit(solution)/shard_map/pallas_call | solution.py:89
  136.8 9.1 %shard_map.113 = bf16[4,2,448,512]{3,2,1,0:T(8,128)(2,1)} custom-call(s32[5]{0:T(128)} %stack.150.pos, bf16[448,1024]{1,0:T(8,128)(2,1)} %get-tuple-element.33.h_ref, bf16[4,4,512,256]{3,2,1,0:T(8,128)(2,1)} %pad_maximum_fusion.a0.a1.c0.c1, bf16[4,4,512,256]{3,2,1,0:T(8,128)(2,1)} %collective-permute-done.16.b0.b1.d0.d1, ...), custom_call_target="tpu_custom_call" | custom-call | flops 3758096384 | bytes 34471956 | tf_op jit(solution)/shard_map/pallas_call | solution.py:89
  146.8 12.3 %collective-permute-done.6 = bf16[448,512]{1,0:T(8,128)(2,1)S(1)} collective-permute-done((bf16[448,512]{1,0:T(8,128)(2,1)S(1)}, bf16[448,512]{1,0:T(8,128)(2,1)S(1)}, u32[]{:S(2)}, u32[]{:S(2)}) %collective-permute-start.6) | collective-permute-done | bytes 458784 | tf_op jit(solution)/shard_map/ppermute | solution.py:22
  160.9 2.4 collective-permute-start.7
  163.3 40.5 %collective-permute-done.8 = bf16[2,448,512]{2,1,0:T(8,128)(2,1)S(1)} collective-permute-done((bf16[2,448,512]{2,1,0:T(8,128)(2,1)S(1)}, bf16[2,448,512]{2,1,0:T(8,128)(2,1)S(1)}, u32[]{:S(2)}, u32[]{:S(2)}) %collective-permute-start.8) | collective-permute-done | bytes 917536 | tf_op jit(solution)/shard_map/ppermute | solution.py:22
  204.0 3.3 collective-permute-start.10
  207.3 9.7 %collective-permute-done.9 = bf16[448,512]{1,0:T(8,128)(2,1)S(1)} collective-permute-done((bf16[448,512]{1,0:T(8,128)(2,1)S(1)}, bf16[448,512]{1,0:T(8,128)(2,1)S(1)}, u32[]{:S(2)}, u32[]{:S(2)}) %collective-permute-start.9) | collective-permute-done | bytes 458784 | tf_op jit(solution)/shard_map/ppermute | solution.py:22
  217.1 2.0 pad_maximum_fusion.2.near_ref.far_ref
  219.1 14.2 %shard_map.114 = (bf16[896,1024]{1,0:T(8,128)(2,1)}, bf16[1024,896]{1,0:T(8,128)(2,1)}) custom-call(s32[5]{0:T(128)} %stack.150.pos, bf16[4,2,448,512]{3,2,1,0:T(8,128)(2,1)} %pad_maximum_fusion.2.near_ref.far_ref, bf16[4,2,448,512]{3,2,1,0:T(8,128)(2,1)} %pad_maximum_fusion.2.near_ref.far_ref, bf16[4,4,512,256]{3,2,1,0:T(8,128)(2,1)} %pad_maximum_fusion.a0.a1.c0.c1, ...), custom_call_target="tpu_custom_call" | custom-call | flops 3758096384 | bytes 44564500 | tf_op jit(solution)/shard_map/pallas_call | solution.py:89
  233.3 15.0 %shard_map.115 = bf16[2,4,4,512,256]{4,3,2,1,0:T(8,128)(2,1)} custom-call(s32[5]{0:T(128)} %stack.150.pos, bf16[1024,896]{1,0:T(8,128)(2,1)} %get-tuple-element.36.g_ref, bf16[4,2,448,512]{3,2,1,0:T(8,128)(2,1)} %bitcast.158, bf16[4,2,448,512]{3,2,1,0:T(8,128)(2,1)} %bitcast.160), custom_call_target="tpu_custom_call" | custom-call | flops 7516192768 | bytes 9175060 | tf_op jit(solution)/shard_map/pallas_call | solution.py:89
  248.3 8.7 %shard_map.116 = bf16[4,2,448,512]{3,2,1,0:T(8,128)(2,1)} custom-call(s32[5]{0:T(128)} %stack.150.pos, bf16[896,1024]{1,0:T(8,128)(2,1)} %get-tuple-element.45.g_ref, bf16[4,4,512,256]{3,2,1,0:T(8,128)(2,1)} %pad_maximum_fusion.1.a0.a1, bf16[4,4,512,256]{3,2,1,0:T(8,128)(2,1)} %collective-permute-done.20.b0.b1, ...), custom_call_target="tpu_custom_call" | custom-call | flops 3758096384 | bytes 18612244 | tf_op jit(solution)/shard_map/pallas_call | solution.py:89
  257.0 4.6 %slice_bitcast_fusion = bf16[4,4,512,256]{3,2,1,0:T(8,128)(2,1)} fusion(bf16[2,4,4,512,256]{4,3,2,1,0:T(8,128)(2,1)} %shard_map.115), kind=kLoop, calls=%fused_computation.4 | loop fusion | bytes 8388608 | tf_op jit(solution)/shard_map/squeeze | solution.py:356
  261.5 8.7 %shard_map.117 = bf16[4,2,448,512]{3,2,1,0:T(8,128)(2,1)} custom-call(s32[5]{0:T(128)} %stack.150.pos, bf16[896,1024]{1,0:T(8,128)(2,1)} %get-tuple-element.45.g_ref, bf16[4,4,512,256]{3,2,1,0:T(8,128)(2,1)} %pad_maximum_fusion.1.a0.a1, bf16[4,4,512,256]{3,2,1,0:T(8,128)(2,1)} %collective-permute-done.20.b0.b1, ...), custom_call_target="tpu_custom_call" | custom-call | flops 3758096384 | bytes 18612244 | tf_op jit(solution)/shard_map/pallas_call | solution.py:89
  270.2 4.8 %fusion = bf16[4,4,512,256]{3,2,1,0:T(8,128)(2,1)S(1)} fusion(bf16[4,4,512,256]{3,2,1,0:T(8,128)(2,1)} %collective-permute-done.21, bf16[2,4,4,512,256]{4,3,2,1,0:T(8,128)(2,1)} %shard_map.115), kind=kLoop, calls=%fused_computation.1 | loop fusion | flops 8388608 | bytes 12582912 | tf_op jit(solution)/shard_map/convert_element_type | solution.py:49
  278.8 2.4 collective-permute-start.23
  285.6 13.8 %reduce-scatter.8.cloned.1.call-done = bf16[1,2,448,512]{3,2,1,0:T(8,128)(2,1)} async-done(((bf16[4,2,448,512]{3,2,1,0:T(8,128)(2,1)}), bf16[1,2,448,512]{3,2,1,0:T(8,128)(2,1)}) %reduce-scatter.8.cloned.1.call-update) | async-done | bytes 917520 | tf_op jit(solution)/shard_map/reduce_scatter | solution.py:265
  299.5 2.2 multiply_bitcast_fusion
  303.9 23.6 %collective-permute-done.23 = bf16[4,512,256]{2,1,0:T(8,128)(2,1)} collective-permute-done((bf16[4,512,256]{2,1,0:T(8,128)(2,1)}, bf16[4,512,256]{2,1,0:T(8,128)(2,1)}, u32[]{:S(2)}, u32[]{:S(2)}) %collective-permute-start.23) | collective-permute-done | bytes 1048608 | tf_op jit(solution)/shard_map/ppermute | solution.py:22
  327.5 2.4 add_convert_fusion
  332.2 2.7 collective-permute-start.27
  340.5 6.1 %collective-permute-done.27 = bf16[512,256]{1,0:T(8,128)(2,1)} collective-permute-done((bf16[512,256]{1,0:T(8,128)(2,1)}, bf16[512,256]{1,0:T(8,128)(2,1)}, u32[]{:S(2)}, u32[]{:S(2)}) %collective-permute-start.27) | collective-permute-done | bytes 262176 | tf_op jit(solution)/shard_map/ppermute | solution.py:22
  (118 shorter events, 59.3 us)
Async XLA Ops:
  7.2 105.7 %all-gather.7.cloned.1.call-start = ((), (), s32[]{:S(2)}) async-start(), calls=%async_computation.7 | async-start | bytes 4587520 | tf_op jit(solution)/shard_map/all_gather | solution.py:268
  14.8 108.9 %all-gather.5.cloned.1.call-start = ((), (), s32[]{:S(2)}) async-start(), calls=%async_computation.6 | async-start | bytes 4587520 | tf_op jit(solution)/shard_map/all_gather | solution.py:268
  14.8 10.0 %collective-permute-start.2 = (bf16[512,256]{1,0:T(8,128)(2,1)S(1)}, bf16[512,256]{1,0:T(8,128)(2,1)S(1)}, u32[]{:S(2)}, u32[]{:S(2)}) collective-permute-start(bf16[512,256]{1,0:T(8,128)(2,1)S(1)} %copy-done.3), channel_id=1, source_target_pairs={{0,64},{64,8},{8,72},{72,0},{1,65},{65,9},{9,73},{73,1},{2,66},{66... | collective-permute-start | bytes 786440 | tf_op jit(solution)/shard_map/ppermute | solution.py:22
  18.1 12.8 %collective-permute-start.1 = (bf16[512,256]{1,0:T(8,128)(2,1)S(1)}, bf16[512,256]{1,0:T(8,128)(2,1)}, u32[]{:S(2)}, u32[]{:S(2)}) collective-permute-start(bf16[512,256]{1,0:T(8,128)(2,1)S(1)} %copy-done.3), channel_id=1, source_target_pairs={{0,8},{64,72},{8,0},{72,64},{1,9},{65,73},{9,1},{73,65},{2,10},{66... | collective-permute-start | bytes 786440 | tf_op jit(solution)/shard_map/ppermute | solution.py:22
  20.0 13.7 %collective-permute-start.3 = (bf16[512,256]{1,0:T(8,128)(2,1)}, bf16[512,256]{1,0:T(8,128)(2,1)}, u32[]{:S(2)}, u32[]{:S(2)}) collective-permute-start(bf16[512,256]{1,0:T(8,128)(2,1)} %param.9), channel_id=1, source_target_pairs={{0,6},{2,0},{4,2},{6,4},{1,7},{3,1},{5,3},{7,5},{8,14},{10,8},{12,... | collective-permute-start | bytes 786440 | tf_op jit(solution)/shard_map/ppermute | solution.py:22
  23.1 11.0 %collective-permute-start.4 = (bf16[512,256]{1,0:T(8,128)(2,1)}, bf16[512,256]{1,0:T(8,128)(2,1)}, u32[]{:S(2)}, u32[]{:S(2)}) collective-permute-start(bf16[512,256]{1,0:T(8,128)(2,1)} %param.9), channel_id=1, source_target_pairs={{0,4},{2,6},{4,0},{6,2},{1,5},{3,7},{5,1},{7,3},{8,12},{10,14},{12... | collective-permute-start | bytes 786440 | tf_op jit(solution)/shard_map/ppermute | solution.py:22
  24.9 12.5 %collective-permute-start.5 = (bf16[512,256]{1,0:T(8,128)(2,1)}, bf16[512,256]{1,0:T(8,128)(2,1)S(1)}, u32[]{:S(2)}, u32[]{:S(2)}) collective-permute-start(bf16[512,256]{1,0:T(8,128)(2,1)} %param.9), channel_id=1, source_target_pairs={{0,2},{2,4},{4,6},{6,0},{1,3},{3,5},{5,7},{7,1},{8,10},{10,12},{12... | collective-permute-start | bytes 786440 | tf_op jit(solution)/shard_map/ppermute | solution.py:22
  38.6 26.2 %collective-permute-start.17 = (bf16[4,512,256]{2,1,0:T(8,128)(2,1)S(1)}, bf16[4,512,256]{2,1,0:T(8,128)(2,1)}, u32[]{:S(2)}, u32[]{:S(2)}) collective-permute-start(bf16[4,512,256]{2,1,0:T(8,128)(2,1)S(1)} %pad_maximum_fusion.3), channel_id=1, source_target_pairs={{0,6},{2,0},{4,2},{6,4},{1,7},{3,1},{5,3},{7,5},{8,14},{10,8},{12,... | collective-permute-start | bytes 3145736 | tf_op jit(solution)/shard_map/ppermute | solution.py:22
  39.3 13.4 %collective-permute-start.11 = (bf16[448,512]{1,0:T(8,128)(2,1)S(1)}, bf16[448,512]{1,0:T(8,128)(2,1)S(1)}, u32[]{:S(2)}, u32[]{:S(2)}) collective-permute-start(bf16[448,512]{1,0:T(8,128)(2,1)S(1)} %copy-done.2), channel_id=1, source_target_pairs={{0,64},{64,0},{1,65},{65,1},{2,66},{66,2},{3,67},{67,3},{4,68},{68... | collective-permute-start | bytes 1376264 | tf_op jit(solution)/shard_map/ppermute | solution.py:22
  39.8 21.1 %collective-permute-start.12 = (bf16[448,512]{1,0:T(8,128)(2,1)S(1)}, bf16[448,512]{1,0:T(8,128)(2,1)S(1)}, u32[]{:S(2)}, u32[]{:S(2)}) collective-permute-start(bf16[448,512]{1,0:T(8,128)(2,1)S(1)} %get-tuple-element.30), channel_id=1, source_target_pairs={{0,64},{64,0},{1,65},{65,1},{2,66},{66,2},{3,67},{67,3},{4,68},{68... | collective-permute-start | bytes 1376264 | tf_op jit(solution)/shard_map/ppermute | solution.py:22
  41.3 27.7 %collective-permute-start.18 = (bf16[4,512,256]{2,1,0:T(8,128)(2,1)S(1)}, bf16[4,512,256]{2,1,0:T(8,128)(2,1)}, u32[]{:S(2)}, u32[]{:S(2)}) collective-permute-start(bf16[4,512,256]{2,1,0:T(8,128)(2,1)S(1)} %pad_maximum_fusion.3), channel_id=1, source_target_pairs={{0,4},{2,6},{4,0},{6,2},{1,5},{3,7},{5,1},{7,3},{8,12},{10,14},{12... | collective-permute-start | bytes 3145736 | tf_op jit(solution)/shard_map/ppermute | solution.py:22
  41.9 47.5 %collective-permute-start.19 = (bf16[4,512,256]{2,1,0:T(8,128)(2,1)S(1)}, bf16[4,512,256]{2,1,0:T(8,128)(2,1)}, u32[]{:S(2)}, u32[]{:S(2)}) collective-permute-start(bf16[4,512,256]{2,1,0:T(8,128)(2,1)S(1)} %pad_maximum_fusion.3), channel_id=1, source_target_pairs={{0,2},{2,4},{4,6},{6,0},{1,3},{3,5},{5,7},{7,1},{8,10},{10,12},{12... | collective-permute-start | bytes 3145736 | tf_op jit(solution)/shard_map/ppermute | solution.py:22
  62.0 220.6 %reduce-scatter.4.cloned.1.call-start = ((), (), s32[]{:S(2)}) async-start(), calls=%async_computation.3 | async-start | bytes 4587520 | tf_op jit(solution)/shard_map/reduce_scatter | solution.py:265
  62.1 31.0 %collective-permute-start.13 = (bf16[4,512,256]{2,1,0:T(8,128)(2,1)S(1)}, bf16[4,512,256]{2,1,0:T(8,128)(2,1)S(1)}, u32[]{:S(2)}, u32[]{:S(2)}) collective-permute-start(bf16[4,512,256]{2,1,0:T(8,128)(2,1)S(1)} %pad_maximum_fusion.4), channel_id=1, source_target_pairs={{0,72},{64,0},{8,64},{72,8},{1,73},{65,1},{9,65},{73,9},{2,74},{66... | collective-permute-start | bytes 3145736 | tf_op jit(solution)/shard_map/ppermute | solution.py:22
  62.8 30.2 %collective-permute-start.14 = (bf16[4,512,256]{2,1,0:T(8,128)(2,1)S(1)}, bf16[4,512,256]{2,1,0:T(8,128)(2,1)S(1)}, u32[]{:S(2)}, u32[]{:S(2)}) collective-permute-start(bf16[4,512,256]{2,1,0:T(8,128)(2,1)S(1)} %pad_maximum_fusion.4), channel_id=1, source_target_pairs={{0,8},{64,72},{8,0},{72,64},{1,9},{65,73},{9,1},{73,65},{2,10},{66... | collective-permute-start | bytes 3145736 | tf_op jit(solution)/shard_map/ppermute | solution.py:22
  64.8 45.2 %collective-permute-start.15 = (bf16[4,512,256]{2,1,0:T(8,128)(2,1)S(1)}, bf16[4,512,256]{2,1,0:T(8,128)(2,1)S(1)}, u32[]{:S(2)}, u32[]{:S(2)}) collective-permute-start(bf16[4,512,256]{2,1,0:T(8,128)(2,1)S(1)} %pad_maximum_fusion.4), channel_id=1, source_target_pairs={{0,64},{64,8},{8,72},{72,0},{1,65},{65,9},{9,73},{73,1},{2,66},{66... | collective-permute-start | bytes 3145736 | tf_op jit(solution)/shard_map/ppermute | solution.py:22
  93.0 19.9 %collective-permute-start.20 = (bf16[4,4,512,256]{3,2,1,0:T(8,128)(2,1)}, bf16[4,4,512,256]{3,2,1,0:T(8,128)(2,1)}, u32[]{:S(2)}, u32[]{:S(2)}) collective-permute-start(bf16[4,4,512,256]{3,2,1,0:T(8,128)(2,1)} %pad_maximum_fusion.1.a0.a1), channel_id=1, source_target_pairs={{0,1},{1,0},{2,3},{3,2},{4,5},{5,4},{6,7},{7,6},{8,9},{9,8},{10,11... | collective-permute-start | bytes 12582920 | tf_op jit(solution)/shard_map/ppermute | solution.py:22
  112.3 24.6 %collective-permute-start.16 = (bf16[4,4,512,256]{3,2,1,0:T(8,128)(2,1)}, bf16[4,4,512,256]{3,2,1,0:T(8,128)(2,1)}, u32[]{:S(2)}, u32[]{:S(2)}) collective-permute-start(bf16[4,4,512,256]{3,2,1,0:T(8,128)(2,1)} %pad_maximum_fusion.a0.a1.c0.c1), channel_id=1, source_target_pairs={{0,1},{1,0},{2,3},{3,2},{4,5},{5,4},{6,7},{7,6},{8,9},{9,8},{10,11... | collective-permute-start | bytes 12582920 | tf_op jit(solution)/shard_map/ppermute | solution.py:22
  146.0 153.5 %reduce-scatter.8.cloned.1.call-start = ((), (), s32[]{:S(2)}) async-start(), calls=%async_computation.5 | async-start | bytes 4587520 | tf_op jit(solution)/shard_map/reduce_scatter | solution.py:265
  146.0 13.0 %collective-permute-start.6 = (bf16[448,512]{1,0:T(8,128)(2,1)S(1)}, bf16[448,512]{1,0:T(8,128)(2,1)S(1)}, u32[]{:S(2)}, u32[]{:S(2)}) collective-permute-start(bf16[448,512]{1,0:T(8,128)(2,1)S(1)} %get-tuple-element.27), channel_id=1, source_target_pairs={{0,64},{64,0},{1,65},{65,1},{2,66},{66,2},{3,67},{67,3},{4,68},{68... | collective-permute-start | bytes 1376264 | tf_op jit(solution)/shard_map/ppermute | solution.py:22
  159.1 44.7 %collective-permute-start.8 = (bf16[2,448,512]{2,1,0:T(8,128)(2,1)S(1)}, bf16[2,448,512]{2,1,0:T(8,128)(2,1)S(1)}, u32[]{:S(2)}, u32[]{:S(2)}) collective-permute-start(bf16[2,448,512]{2,1,0:T(8,128)(2,1)S(1)} %get-tuple-element.76), channel_id=1, source_target_pairs={{0,16},{16,32},{32,48},{48,0},{1,17},{17,33},{33,49},{49,1},{2,18}... | collective-permute-start | bytes 2752520 | tf_op jit(solution)/shard_map/ppermute | solution.py:22
  160.9 43.1 %collective-permute-start.7 = (bf16[2,448,512]{2,1,0:T(8,128)(2,1)S(1)}, bf16[2,448,512]{2,1,0:T(8,128)(2,1)S(1)}, u32[]{:S(2)}, u32[]{:S(2)}) collective-permute-start(bf16[2,448,512]{2,1,0:T(8,128)(2,1)S(1)} %get-tuple-element.76), channel_id=1, source_target_pairs={{0,48},{16,0},{32,16},{48,32},{1,49},{17,1},{33,17},{49,33},{2,50}... | collective-permute-start | bytes 2752520 | tf_op jit(solution)/shard_map/ppermute | solution.py:22
  203.9 13.1 %collective-permute-start.9 = (bf16[448,512]{1,0:T(8,128)(2,1)S(1)}, bf16[448,512]{1,0:T(8,128)(2,1)S(1)}, u32[]{:S(2)}, u32[]{:S(2)}) collective-permute-start(bf16[448,512]{1,0:T(8,128)(2,1)S(1)} %slice_bitcast_fusion.8), channel_id=1, source_target_pairs={{0,16},{16,32},{32,48},{48,0},{1,17},{17,33},{33,49},{49,1},{2,18}... | collective-permute-start | bytes 1376264 | tf_op jit(solution)/shard_map/ppermute | solution.py:22
  204.0 13.0 %collective-permute-start.10 = (bf16[448,512]{1,0:T(8,128)(2,1)S(1)}, bf16[448,512]{1,0:T(8,128)(2,1)S(1)}, u32[]{:S(2)}, u32[]{:S(2)}) collective-permute-start(bf16[448,512]{1,0:T(8,128)(2,1)S(1)} %slice_bitcast_fusion.7), channel_id=1, source_target_pairs={{0,48},{16,0},{32,16},{48,32},{1,49},{17,1},{33,17},{49,33},{2,50}... | collective-permute-start | bytes 1376264 | tf_op jit(solution)/shard_map/ppermute | solution.py:22
  256.9 91.7 %reduce-scatter.6.cloned.1.call-start = ((), (), s32[]{:S(2)}) async-start(), calls=%async_computation.4 | async-start | bytes 4587520 | tf_op jit(solution)/shard_map/reduce_scatter | solution.py:265
  276.9 27.0 %collective-permute-start.22 = (bf16[4,512,256]{2,1,0:T(8,128)(2,1)}, bf16[4,512,256]{2,1,0:T(8,128)(2,1)S(1)}, u32[]{:S(2)}, u32[]{:S(2)}) collective-permute-start(bf16[4,512,256]{2,1,0:T(8,128)(2,1)} %get-tuple-element.60), channel_id=1, source_target_pairs={{0,2},{2,4},{4,6},{6,0},{1,3},{3,5},{5,7},{7,1},{8,10},{10,12},{12... | collective-permute-start | bytes 3145736 | tf_op jit(solution)/shard_map/ppermute | solution.py:22
  278.8 48.7 %collective-permute-start.23 = (bf16[4,512,256]{2,1,0:T(8,128)(2,1)}, bf16[4,512,256]{2,1,0:T(8,128)(2,1)}, u32[]{:S(2)}, u32[]{:S(2)}) collective-permute-start(bf16[4,512,256]{2,1,0:T(8,128)(2,1)} %get-tuple-element.59), channel_id=1, source_target_pairs={{0,4},{2,6},{4,0},{6,2},{1,5},{3,7},{5,1},{7,3},{8,12},{10,14},{12... | collective-permute-start | bytes 3145736 | tf_op jit(solution)/shard_map/ppermute | solution.py:22
  281.1 46.3 %collective-permute-start.24 = (bf16[4,512,256]{2,1,0:T(8,128)(2,1)}, bf16[4,512,256]{2,1,0:T(8,128)(2,1)}, u32[]{:S(2)}, u32[]{:S(2)}) collective-permute-start(bf16[4,512,256]{2,1,0:T(8,128)(2,1)} %get-tuple-element.58), channel_id=1, source_target_pairs={{0,6},{2,0},{4,2},{6,4},{1,7},{3,1},{5,3},{7,5},{8,14},{10,8},{12,... | collective-permute-start | bytes 3145736 | tf_op jit(solution)/shard_map/ppermute | solution.py:22
  283.8 43.6 %collective-permute-start.25 = (bf16[448,512]{1,0:T(8,128)(2,1)S(1)}, bf16[448,512]{1,0:T(8,128)(2,1)S(1)}, u32[]{:S(2)}, u32[]{:S(2)}) collective-permute-start(bf16[448,512]{1,0:T(8,128)(2,1)S(1)} %get-tuple-element.66), channel_id=1, source_target_pairs={{0,64},{64,0},{1,65},{65,1},{2,66},{66,2},{3,67},{67,3},{4,68},{68... | collective-permute-start | bytes 1376264 | tf_op jit(solution)/shard_map/ppermute | solution.py:22
  301.6 47.0 %collective-permute-start.29 = (bf16[2,448,512]{2,1,0:T(8,128)(2,1)}, bf16[2,448,512]{2,1,0:T(8,128)(2,1)}, u32[]{:S(2)}, u32[]{:S(2)}) collective-permute-start(bf16[2,448,512]{2,1,0:T(8,128)(2,1)} %multiply_bitcast_fusion), channel_id=1, source_target_pairs={{0,64},{64,0},{1,65},{65,1},{2,66},{66,2},{3,67},{67,3},{4,68},{68... | collective-permute-start | bytes 2752520 | tf_op jit(solution)/shard_map/ppermute | solution.py:22
  332.2 14.5 %collective-permute-start.27 = (bf16[512,256]{1,0:T(8,128)(2,1)}, bf16[512,256]{1,0:T(8,128)(2,1)}, u32[]{:S(2)}, u32[]{:S(2)}) collective-permute-start(bf16[512,256]{1,0:T(8,128)(2,1)} %get-tuple-element.64), channel_id=1, source_target_pairs={{0,8},{64,72},{8,0},{72,64},{1,9},{65,73},{9,1},{73,65},{2,10},{66... | collective-permute-start | bytes 786440 | tf_op jit(solution)/shard_map/ppermute | solution.py:22
  334.9 11.8 %collective-permute-start.28 = (bf16[512,256]{1,0:T(8,128)(2,1)}, bf16[512,256]{1,0:T(8,128)(2,1)}, u32[]{:S(2)}, u32[]{:S(2)}) collective-permute-start(bf16[512,256]{1,0:T(8,128)(2,1)} %get-tuple-element.63), channel_id=1, source_target_pairs={{0,72},{64,0},{8,64},{72,8},{1,73},{65,1},{9,65},{73,9},{2,74},{66... | collective-permute-start | bytes 786440 | tf_op jit(solution)/shard_map/ppermute | solution.py:22
  (10 other events, 102.7 us)
Sparse Core Ops, SparseCore 0:
  14.9 46.5 all-gather.6
  63.7 44.1 all-gather.4
  146.1 62.2 reduce-scatter.3
  257.1 42.3 reduce-scatter.7
  301.7 42.3 reduce-scatter.5

commit v2 on v1

--- a/solution.py
+++ b/solution.py
@@ -212,31 +212,33 @@
         out_ref[0, place, :, cols] = term.astype(BF16)
 
 
-def token_grads_kernel(pos, g_ref, near_ref, far_ref, out_ref):
+def token_grads_kernel(pos, g_ref, near_ref, far_ref, own_ref, other_ref):
     here, far = pos[2], pl.program_id(1)
     near_w, far_w = (ref.at[0].reshape(2 * RANGE, 512)[...] for ref in (near_ref, far_ref))
     w = jnp.where(far == 0, near_w, far_w)
     term = lax.dot_general(g_ref[...], w, NN, preferred_element_type=F32).astype(BF16)
+    low, high = term[:, :256], term[:, 256:]
+    own, other = jnp.where(here == 0, low, high), jnp.where(here == 0, high, low)
     for xl in (0, 1):
         place = turn_x(pos, far ^ pos[3], xl)
-        out_ref[here, 0, place] = term[xl * 512 : (xl + 1) * 512, :256]
-        out_ref[1 - here, 0, place] = term[xl * 512 : (xl + 1) * 512, 256:]
+        own_ref[0, place] = own[xl * 512 : (xl + 1) * 512]
+        other_ref[0, place] = other[xl * 512 : (xl + 1) * 512]
 
 
 def token_grads(pos, turned, near, far_w):
     def place(z, far, pos):
-        return (0, turn_y(pos, z), 0, 0, 0)
+        return (turn_y(pos, z), 0, 0, 0)
 
     return call(
         token_grads_kernel,
         (4, 2),
         [whole(turned.shape), by_z(2, 0), by_z(2, 0)],
-        [((2, 4, 4, 512, 256), BF16)],
-        [pl.BlockSpec((2, 1, 4, 512, 256), place)],
+        [((4, 4, 512, 256), BF16)] * 2,
+        [pl.BlockSpec((1, 4, 512, 256), place)] * 2,
         [],
         2 * FLOPS,
         (pos, turned, near, far_w),
-    )[0]
+    )
 
 
 def on_device(

time: 363 us -> 358 us (0.986)
  local copies, waits for them, and re-layouts: 22.3 us -> 17.2 us
    ppermute x30, waiting for transfers between devices: 164 us -> 159 us  [shift(): lax.ppermute(value, axis, [(name(i), name((i + step) % size)) for i in ra...]
    squeeze x1 -> x0, local copies, waits for them, and re-layouts: 4.55 us -> none  [on_device(): core_part = shift(parts[1], 'c', 2, 1)]
    reduce_scatter x3, waiting for transfers between devices: 13.8 us -> 17.5 us  [over_z_sum(): return lax.psum_scatter(rows, 'z', scatter_dimension=0, tiled=True)[0]]
  transfers between devices with their start and end apart: 35 -> 35, of which waited for: 18 -> 17; matrix products, arithmetic and copies ran while one was open for 10% -> 9% of each run, Pallas kernels for 19% -> 20%
where the time goes in v2:
time: 358 us; the launch traced here: 356 us
  waiting for transfers between devices  176 us (49%)
  Pallas kernels  79.6 us (22%)
  starting transfers between devices  40.2 us (11%)
  other arithmetic  28.9 us (8%)
  local copies, waits for them, and re-layouts  17.2 us (5%)
  between operations  14.1 us (4%)
    ppermute x30, waiting for transfers between devices, shift(): lax.ppermute(value, axis, [(name(i), name((i + step) % size)) for i in ra...  159 us
    pallas_call x7, Pallas kernels, call(): pl.pallas_call(kernel, out_shape=[jax.ShapeDtypeStruct(shape, kind) for s...  79.6 us
    ppermute x30, starting transfers between devices, shift(): lax.ppermute(value, axis, [(name(i), name((i + step) % size)) for i in ra...  40 us
    reduce_scatter x3, waiting for transfers between devices, over_z_sum(): return lax.psum_scatter(rows, 'z', scatter_dimension=0, tiled=True)[0]  17.5 us
    convert_element_type x3, other arithmetic, total_of(): return sum((b.astype(F32) for b in blocks)).astype(BF16)  9.07 us
    unnamed x20, local copies, waits for them, and re-layouts  7.3 us
  transfers between devices with their start and end apart: 35, of which 17 were waited for; matrix products, arithmetic and copies ran while one was open for 9% of the time, Pallas kernels for 20%

profile of v2, /device:TPU:0, one launch (start us, length us, event | category | flops | bytes accessed | tf_op | source)
XLA Modules:
  0.0 356.3 jit_solution(16609241939665696946)
XLA Ops:
  20.0 3.0 collective-permute-start.3
  26.1 4.9 %collective-permute-done.1 = bf16[512,256]{1,0:T(8,128)(2,1)} collective-permute-done((bf16[512,256]{1,0:T(8,128)(2,1)S(1)}, bf16[512,256]{1,0:T(8,128)(2,1)}, u32[]{:S(2)}, u32[]{:S(2)}) %collective-permute-start.1) | collective-permute-done | bytes 262176 | tf_op jit(solution)/shard_map/ppermute | solution.py:22
  34.1 3.2 collective-permute-done.5
  42.7 9.9 %collective-permute-done.11 = bf16[448,512]{1,0:T(8,128)(2,1)S(1)} collective-permute-done((bf16[448,512]{1,0:T(8,128)(2,1)S(1)}, bf16[448,512]{1,0:T(8,128)(2,1)S(1)}, u32[]{:S(2)}, u32[]{:S(2)}) %collective-permute-start.11) | collective-permute-done | bytes 458784 | tf_op jit(solution)/shard_map/ppermute | solution.py:22
  52.6 8.3 %collective-permute-done.12 = bf16[448,512]{1,0:T(8,128)(2,1)S(1)} collective-permute-done((bf16[448,512]{1,0:T(8,128)(2,1)S(1)}, bf16[448,512]{1,0:T(8,128)(2,1)S(1)}, u32[]{:S(2)}, u32[]{:S(2)}) %collective-permute-start.12) | collective-permute-done | bytes 458784 | tf_op jit(solution)/shard_map/ppermute | solution.py:22
  65.4 3.6 %collective-permute-done.18 = bf16[4,512,256]{2,1,0:T(8,128)(2,1)} collective-permute-done((bf16[4,512,256]{2,1,0:T(8,128)(2,1)S(1)}, bf16[4,512,256]{2,1,0:T(8,128)(2,1)}, u32[]{:S(2)}, u32[]{:S(2)}) %collective-permute-start.18) | collective-permute-done | bytes 1048608 | tf_op jit(solution)/shard_map/ppermute | solution.py:22
  69.0 20.4 %collective-permute-done.19 = bf16[4,512,256]{2,1,0:T(8,128)(2,1)} collective-permute-done((bf16[4,512,256]{2,1,0:T(8,128)(2,1)S(1)}, bf16[4,512,256]{2,1,0:T(8,128)(2,1)}, u32[]{:S(2)}, u32[]{:S(2)}) %collective-permute-start.19) | collective-permute-done | bytes 1048608 | tf_op jit(solution)/shard_map/ppermute | solution.py:22
  89.3 3.7 %pad_maximum_fusion.1.a0.a1 = bf16[4,4,512,256]{3,2,1,0:T(8,128)(2,1)} fusion(bf16[1,4,512,256]{3,2,1,0:T(8,128)(2,1)} %bitcast.42, bf16[1,4,512,256]{3,2,1,0:T(8,128)(2,1)} %bitcast.41, bf16[1,4,512,256]{3,2,1,0:T(8,128)(2,1)} %bitcast.40, bf16[1,4,512,256]{3,2,1,0:T(8,128)(2,1)S(1)} %bitcast.147), kind=kLoop, calls=%fused_computation.2 | loop fusion | flops 6291456 | bytes 8388608 | tf_op jit(solution)/shard_map/stack | solution.py:288
  93.0 17.0 %collective-permute-done.15 = bf16[4,512,256]{2,1,0:T(8,128)(2,1)S(1)} collective-permute-done((bf16[4,512,256]{2,1,0:T(8,128)(2,1)S(1)}, bf16[4,512,256]{2,1,0:T(8,128)(2,1)S(1)}, u32[]{:S(2)}, u32[]{:S(2)}) %collective-permute-start.15) | collective-permute-done | bytes 1048608 | tf_op jit(solution)/shard_map/ppermute | solution.py:22
  110.0 2.3 pad_maximum_fusion.a0.a1.c0.c1
  112.9 10.8 %shard_map.111.near_ref = f32[896,1024]{1,0:T(8,128)} custom-call(s32[5]{0:T(128)} %stack.150.pos, bf16[4,2,448,512]{3,2,1,0:T(8,128)(2,1)} %bitcast.152, bf16[4,4,512,256]{3,2,1,0:T(8,128)(2,1)} %pad_maximum_fusion.1.a0.a1, bf16[4,4,512,256]{3,2,1,0:T(8,128)(2,1)} %collective-permute-done.20.b0.b1, bf16[4,4,512,256]{3,2,1,0:T(8,128)(2,1)} %pad_maximum_fusion.1.a0.a1, ...), custom_call_target="tpu_custom_call" | custom-call | flops 3758096384 | bytes 20447252 | tf_op jit(solution)/shard_map/pallas_call | solution.py:89
  123.8 13.2 %shard_map.112 = (f32[896,1024]{1,0:T(8,128)}, bf16[448,1024]{1,0:T(8,128)(2,1)}) custom-call(s32[5]{0:T(128)} %stack.150.pos, bf16[4,2,448,512]{3,2,1,0:T(8,128)(2,1)} %bitcast.154, bf16[4,4,512,256]{3,2,1,0:T(8,128)(2,1)} %pad_maximum_fusion.1.a0.a1, bf16[4,4,512,256]{3,2,1,0:T(8,128)(2,1)} %collective-permute-done.20.b0.b1, ...), custom_call_target="tpu_custom_call" | custom-call | flops 3758096384 | bytes 24117268 | tf_op jit(solution)/shard_map/pallas_call | solution.py:89
  137.0 9.1 %shard_map.113 = bf16[4,2,448,512]{3,2,1,0:T(8,128)(2,1)} custom-call(s32[5]{0:T(128)} %stack.150.pos, bf16[448,1024]{1,0:T(8,128)(2,1)} %get-tuple-element.36.h_ref, bf16[4,4,512,256]{3,2,1,0:T(8,128)(2,1)} %pad_maximum_fusion.a0.a1.c0.c1, bf16[4,4,512,256]{3,2,1,0:T(8,128)(2,1)} %collective-permute-done.16.b0.b1.d0.d1, ...), custom_call_target="tpu_custom_call" | custom-call | flops 3758096384 | bytes 34471956 | tf_op jit(solution)/shard_map/pallas_call | solution.py:89
  146.9 12.3 %collective-permute-done.6 = bf16[448,512]{1,0:T(8,128)(2,1)S(1)} collective-permute-done((bf16[448,512]{1,0:T(8,128)(2,1)S(1)}, bf16[448,512]{1,0:T(8,128)(2,1)S(1)}, u32[]{:S(2)}, u32[]{:S(2)}) %collective-permute-start.6) | collective-permute-done | bytes 458784 | tf_op jit(solution)/shard_map/ppermute | solution.py:22
  161.0 2.4 collective-permute-start.7
  163.4 40.5 %collective-permute-done.8 = bf16[2,448,512]{2,1,0:T(8,128)(2,1)S(1)} collective-permute-done((bf16[2,448,512]{2,1,0:T(8,128)(2,1)S(1)}, bf16[2,448,512]{2,1,0:T(8,128)(2,1)S(1)}, u32[]{:S(2)}, u32[]{:S(2)}) %collective-permute-start.8) | collective-permute-done | bytes 917536 | tf_op jit(solution)/shard_map/ppermute | solution.py:22
  204.1 3.3 collective-permute-start.10
  207.3 9.7 %collective-permute-done.9 = bf16[448,512]{1,0:T(8,128)(2,1)S(1)} collective-permute-done((bf16[448,512]{1,0:T(8,128)(2,1)S(1)}, bf16[448,512]{1,0:T(8,128)(2,1)S(1)}, u32[]{:S(2)}, u32[]{:S(2)}) %collective-permute-start.9) | collective-permute-done | bytes 458784 | tf_op jit(solution)/shard_map/ppermute | solution.py:22
  217.1 2.0 pad_maximum_fusion.2.near_ref.far_ref
  219.1 14.1 %shard_map.114 = (bf16[896,1024]{1,0:T(8,128)(2,1)}, bf16[1024,896]{1,0:T(8,128)(2,1)}) custom-call(s32[5]{0:T(128)} %stack.150.pos, bf16[4,2,448,512]{3,2,1,0:T(8,128)(2,1)} %pad_maximum_fusion.2.near_ref.far_ref, bf16[4,2,448,512]{3,2,1,0:T(8,128)(2,1)} %pad_maximum_fusion.2.near_ref.far_ref, bf16[4,4,512,256]{3,2,1,0:T(8,128)(2,1)} %pad_maximum_fusion.a0.a1.c0.c1, ...), custom_call_target="tpu_custom_call" | custom-call | flops 3758096384 | bytes 44564500 | tf_op jit(solution)/shard_map/pallas_call | solution.py:89
  233.3 15.0 %shard_map.115 = (bf16[4,4,512,256]{3,2,1,0:T(8,128)(2,1)}, bf16[4,4,512,256]{3,2,1,0:T(8,128)(2,1)}) custom-call(s32[5]{0:T(128)} %stack.150.pos, bf16[1024,896]{1,0:T(8,128)(2,1)} %get-tuple-element.39.g_ref, bf16[4,2,448,512]{3,2,1,0:T(8,128)(2,1)} %bitcast.153, bf16[4,2,448,512]{3,2,1,0:T(8,128)(2,1)} %bitcast.155), custom_call_target="tpu_custom_call" | custom-call | flops 7516192768 | bytes 9175060 | tf_op jit(solution)/shard_map/pallas_call | solution.py:89
  248.2 8.7 %shard_map.116 = bf16[4,2,448,512]{3,2,1,0:T(8,128)(2,1)} custom-call(s32[5]{0:T(128)} %stack.150.pos, bf16[896,1024]{1,0:T(8,128)(2,1)} %get-tuple-element.51.g_ref, bf16[4,4,512,256]{3,2,1,0:T(8,128)(2,1)} %pad_maximum_fusion.1.a0.a1, bf16[4,4,512,256]{3,2,1,0:T(8,128)(2,1)} %collective-permute-done.20.b0.b1, ...), custom_call_target="tpu_custom_call" | custom-call | flops 3758096384 | bytes 18612244 | tf_op jit(solution)/shard_map/pallas_call | solution.py:89
  257.3 8.8 %shard_map.117 = bf16[4,2,448,512]{3,2,1,0:T(8,128)(2,1)} custom-call(s32[5]{0:T(128)} %stack.150.pos, bf16[896,1024]{1,0:T(8,128)(2,1)} %get-tuple-element.51.g_ref, bf16[4,4,512,256]{3,2,1,0:T(8,128)(2,1)} %pad_maximum_fusion.1.a0.a1, bf16[4,4,512,256]{3,2,1,0:T(8,128)(2,1)} %collective-permute-done.20.b0.b1, ...), custom_call_target="tpu_custom_call" | custom-call | flops 3758096384 | bytes 18612244 | tf_op jit(solution)/shard_map/pallas_call | solution.py:89
  266.1 4.7 %add_convert_fusion = bf16[4,4,512,256]{3,2,1,0:T(8,128)(2,1)S(1)} fusion(bf16[4,4,512,256]{3,2,1,0:T(8,128)(2,1)} %collective-permute-done.21, bf16[4,4,512,256]{3,2,1,0:T(8,128)(2,1)} %get-tuple-element.43), kind=kLoop, calls=%fused_computation | loop fusion | flops 8388608 | bytes 12582912 | tf_op jit(solution)/shard_map/convert_element_type | solution.py:49
  274.4 2.2 collective-permute-start.23
  278.1 2.0 slice_bitcast_fusion.4
  281.8 17.5 %reduce-scatter.8.cloned.1.call-done = bf16[1,2,448,512]{3,2,1,0:T(8,128)(2,1)} async-done(((bf16[4,2,448,512]{3,2,1,0:T(8,128)(2,1)}), bf16[1,2,448,512]{3,2,1,0:T(8,128)(2,1)}) %reduce-scatter.8.cloned.1.call-update) | async-done | bytes 917520 | tf_op jit(solution)/shard_map/reduce_scatter | solution.py:267
  299.3 2.2 multiply_bitcast_fusion
  303.0 20.0 %collective-permute-done.23 = bf16[4,512,256]{2,1,0:T(8,128)(2,1)} collective-permute-done((bf16[4,512,256]{2,1,0:T(8,128)(2,1)}, bf16[4,512,256]{2,1,0:T(8,128)(2,1)}, u32[]{:S(2)}, u32[]{:S(2)}) %collective-permute-start.23) | collective-permute-done | bytes 1048608 | tf_op jit(solution)/shard_map/ppermute | solution.py:22
  323.0 2.4 add_convert_fusion.1
  327.7 2.7 collective-permute-start.27
  336.1 6.2 %collective-permute-done.27 = bf16[512,256]{1,0:T(8,128)(2,1)} collective-permute-done((bf16[512,256]{1,0:T(8,128)(2,1)}, bf16[512,256]{1,0:T(8,128)(2,1)}, u32[]{:S(2)}, u32[]{:S(2)}) %collective-permute-start.27) | collective-permute-done | bytes 262176 | tf_op jit(solution)/shard_map/ppermute | solution.py:22
  (117 shorter events, 56.3 us)
Async XLA Ops:
  7.2 105.8 %all-gather.7.cloned.1.call-start = ((), (), s32[]{:S(2)}) async-start(), calls=%async_computation.7 | async-start | bytes 4587520 | tf_op jit(solution)/shard_map/all_gather | solution.py:270
  14.8 109.0 %all-gather.5.cloned.1.call-start = ((), (), s32[]{:S(2)}) async-start(), calls=%async_computation.6 | async-start | bytes 4587520 | tf_op jit(solution)/shard_map/all_gather | solution.py:270
  14.8 10.0 %collective-permute-start.2 = (bf16[512,256]{1,0:T(8,128)(2,1)S(1)}, bf16[512,256]{1,0:T(8,128)(2,1)S(1)}, u32[]{:S(2)}, u32[]{:S(2)}) collective-permute-start(bf16[512,256]{1,0:T(8,128)(2,1)S(1)} %copy-done.3), channel_id=1, source_target_pairs={{0,64},{64,8},{8,72},{72,0},{1,65},{65,9},{9,73},{73,1},{2,66},{66... | collective-permute-start | bytes 786440 | tf_op jit(solution)/shard_map/ppermute | solution.py:22
  18.1 12.8 %collective-permute-start.1 = (bf16[512,256]{1,0:T(8,128)(2,1)S(1)}, bf16[512,256]{1,0:T(8,128)(2,1)}, u32[]{:S(2)}, u32[]{:S(2)}) collective-permute-start(bf16[512,256]{1,0:T(8,128)(2,1)S(1)} %copy-done.3), channel_id=1, source_target_pairs={{0,8},{64,72},{8,0},{72,64},{1,9},{65,73},{9,1},{73,65},{2,10},{66... | collective-permute-start | bytes 786440 | tf_op jit(solution)/shard_map/ppermute | solution.py:22
  20.0 13.7 %collective-permute-start.3 = (bf16[512,256]{1,0:T(8,128)(2,1)}, bf16[512,256]{1,0:T(8,128)(2,1)}, u32[]{:S(2)}, u32[]{:S(2)}) collective-permute-start(bf16[512,256]{1,0:T(8,128)(2,1)} %param.9), channel_id=1, source_target_pairs={{0,6},{2,0},{4,2},{6,4},{1,7},{3,1},{5,3},{7,5},{8,14},{10,8},{12,... | collective-permute-start | bytes 786440 | tf_op jit(solution)/shard_map/ppermute | solution.py:22
  23.1 11.0 %collective-permute-start.4 = (bf16[512,256]{1,0:T(8,128)(2,1)}, bf16[512,256]{1,0:T(8,128)(2,1)}, u32[]{:S(2)}, u32[]{:S(2)}) collective-permute-start(bf16[512,256]{1,0:T(8,128)(2,1)} %param.9), channel_id=1, source_target_pairs={{0,4},{2,6},{4,0},{6,2},{1,5},{3,7},{5,1},{7,3},{8,12},{10,14},{12... | collective-permute-start | bytes 786440 | tf_op jit(solution)/shard_map/ppermute | solution.py:22
  24.9 12.5 %collective-permute-start.5 = (bf16[512,256]{1,0:T(8,128)(2,1)}, bf16[512,256]{1,0:T(8,128)(2,1)S(1)}, u32[]{:S(2)}, u32[]{:S(2)}) collective-permute-start(bf16[512,256]{1,0:T(8,128)(2,1)} %param.9), channel_id=1, source_target_pairs={{0,2},{2,4},{4,6},{6,0},{1,3},{3,5},{5,7},{7,1},{8,10},{10,12},{12... | collective-permute-start | bytes 786440 | tf_op jit(solution)/shard_map/ppermute | solution.py:22
  38.6 26.2 %collective-permute-start.17 = (bf16[4,512,256]{2,1,0:T(8,128)(2,1)S(1)}, bf16[4,512,256]{2,1,0:T(8,128)(2,1)}, u32[]{:S(2)}, u32[]{:S(2)}) collective-permute-start(bf16[4,512,256]{2,1,0:T(8,128)(2,1)S(1)} %pad_maximum_fusion.3), channel_id=1, source_target_pairs={{0,6},{2,0},{4,2},{6,4},{1,7},{3,1},{5,3},{7,5},{8,14},{10,8},{12,... | collective-permute-start | bytes 3145736 | tf_op jit(solution)/shard_map/ppermute | solution.py:22
  39.3 13.4 %collective-permute-start.11 = (bf16[448,512]{1,0:T(8,128)(2,1)S(1)}, bf16[448,512]{1,0:T(8,128)(2,1)S(1)}, u32[]{:S(2)}, u32[]{:S(2)}) collective-permute-start(bf16[448,512]{1,0:T(8,128)(2,1)S(1)} %copy-done.2), channel_id=1, source_target_pairs={{0,64},{64,0},{1,65},{65,1},{2,66},{66,2},{3,67},{67,3},{4,68},{68... | collective-permute-start | bytes 1376264 | tf_op jit(solution)/shard_map/ppermute | solution.py:22
  39.8 21.1 %collective-permute-start.12 = (bf16[448,512]{1,0:T(8,128)(2,1)S(1)}, bf16[448,512]{1,0:T(8,128)(2,1)S(1)}, u32[]{:S(2)}, u32[]{:S(2)}) collective-permute-start(bf16[448,512]{1,0:T(8,128)(2,1)S(1)} %get-tuple-element.33), channel_id=1, source_target_pairs={{0,64},{64,0},{1,65},{65,1},{2,66},{66,2},{3,67},{67,3},{4,68},{68... | collective-permute-start | bytes 1376264 | tf_op jit(solution)/shard_map/ppermute | solution.py:22
  41.3 27.7 %collective-permute-start.18 = (bf16[4,512,256]{2,1,0:T(8,128)(2,1)S(1)}, bf16[4,512,256]{2,1,0:T(8,128)(2,1)}, u32[]{:S(2)}, u32[]{:S(2)}) collective-permute-start(bf16[4,512,256]{2,1,0:T(8,128)(2,1)S(1)} %pad_maximum_fusion.3), channel_id=1, source_target_pairs={{0,4},{2,6},{4,0},{6,2},{1,5},{3,7},{5,1},{7,3},{8,12},{10,14},{12... | collective-permute-start | bytes 3145736 | tf_op jit(solution)/shard_map/ppermute | solution.py:22
  41.9 47.5 %collective-permute-start.19 = (bf16[4,512,256]{2,1,0:T(8,128)(2,1)S(1)}, bf16[4,512,256]{2,1,0:T(8,128)(2,1)}, u32[]{:S(2)}, u32[]{:S(2)}) collective-permute-start(bf16[4,512,256]{2,1,0:T(8,128)(2,1)S(1)} %pad_maximum_fusion.3), channel_id=1, source_target_pairs={{0,2},{2,4},{4,6},{6,0},{1,3},{3,5},{5,7},{7,1},{8,10},{10,12},{12... | collective-permute-start | bytes 3145736 | tf_op jit(solution)/shard_map/ppermute | solution.py:22
  62.0 216.1 %reduce-scatter.4.cloned.1.call-start = ((), (), s32[]{:S(2)}) async-start(), calls=%async_computation.3 | async-start | bytes 4587520 | tf_op jit(solution)/shard_map/reduce_scatter | solution.py:267
  62.1 30.9 %collective-permute-start.13 = (bf16[4,512,256]{2,1,0:T(8,128)(2,1)S(1)}, bf16[4,512,256]{2,1,0:T(8,128)(2,1)S(1)}, u32[]{:S(2)}, u32[]{:S(2)}) collective-permute-start(bf16[4,512,256]{2,1,0:T(8,128)(2,1)S(1)} %pad_maximum_fusion.4), channel_id=1, source_target_pairs={{0,72},{64,0},{8,64},{72,8},{1,73},{65,1},{9,65},{73,9},{2,74},{66... | collective-permute-start | bytes 3145736 | tf_op jit(solution)/shard_map/ppermute | solution.py:22
  62.8 30.2 %collective-permute-start.14 = (bf16[4,512,256]{2,1,0:T(8,128)(2,1)S(1)}, bf16[4,512,256]{2,1,0:T(8,128)(2,1)S(1)}, u32[]{:S(2)}, u32[]{:S(2)}) collective-permute-start(bf16[4,512,256]{2,1,0:T(8,128)(2,1)S(1)} %pad_maximum_fusion.4), channel_id=1, source_target_pairs={{0,8},{64,72},{8,0},{72,64},{1,9},{65,73},{9,1},{73,65},{2,10},{66... | collective-permute-start | bytes 3145736 | tf_op jit(solution)/shard_map/ppermute | solution.py:22
  64.8 45.2 %collective-permute-start.15 = (bf16[4,512,256]{2,1,0:T(8,128)(2,1)S(1)}, bf16[4,512,256]{2,1,0:T(8,128)(2,1)S(1)}, u32[]{:S(2)}, u32[]{:S(2)}) collective-permute-start(bf16[4,512,256]{2,1,0:T(8,128)(2,1)S(1)} %pad_maximum_fusion.4), channel_id=1, source_target_pairs={{0,64},{64,8},{8,72},{72,0},{1,65},{65,9},{9,73},{73,1},{2,66},{66... | collective-permute-start | bytes 3145736 | tf_op jit(solution)/shard_map/ppermute | solution.py:22
  93.0 19.9 %collective-permute-start.20 = (bf16[4,4,512,256]{3,2,1,0:T(8,128)(2,1)}, bf16[4,4,512,256]{3,2,1,0:T(8,128)(2,1)}, u32[]{:S(2)}, u32[]{:S(2)}) collective-permute-start(bf16[4,4,512,256]{3,2,1,0:T(8,128)(2,1)} %pad_maximum_fusion.1.a0.a1), channel_id=1, source_target_pairs={{0,1},{1,0},{2,3},{3,2},{4,5},{5,4},{6,7},{7,6},{8,9},{9,8},{10,11... | collective-permute-start | bytes 12582920 | tf_op jit(solution)/shard_map/ppermute | solution.py:22
  112.3 24.6 %collective-permute-start.16 = (bf16[4,4,512,256]{3,2,1,0:T(8,128)(2,1)}, bf16[4,4,512,256]{3,2,1,0:T(8,128)(2,1)}, u32[]{:S(2)}, u32[]{:S(2)}) collective-permute-start(bf16[4,4,512,256]{3,2,1,0:T(8,128)(2,1)} %pad_maximum_fusion.a0.a1.c0.c1), channel_id=1, source_target_pairs={{0,1},{1,0},{2,3},{3,2},{4,5},{5,4},{6,7},{7,6},{8,9},{9,8},{10,11... | collective-permute-start | bytes 12582920 | tf_op jit(solution)/shard_map/ppermute | solution.py:22
  146.1 153.2 %reduce-scatter.8.cloned.1.call-start = ((), (), s32[]{:S(2)}) async-start(), calls=%async_computation.5 | async-start | bytes 4587520 | tf_op jit(solution)/shard_map/reduce_scatter | solution.py:267
  146.1 13.0 %collective-permute-start.6 = (bf16[448,512]{1,0:T(8,128)(2,1)S(1)}, bf16[448,512]{1,0:T(8,128)(2,1)S(1)}, u32[]{:S(2)}, u32[]{:S(2)}) collective-permute-start(bf16[448,512]{1,0:T(8,128)(2,1)S(1)} %get-tuple-element.30), channel_id=1, source_target_pairs={{0,64},{64,0},{1,65},{65,1},{2,66},{66,2},{3,67},{67,3},{4,68},{68... | collective-permute-start | bytes 1376264 | tf_op jit(solution)/shard_map/ppermute | solution.py:22
  159.2 44.7 %collective-permute-start.8 = (bf16[2,448,512]{2,1,0:T(8,128)(2,1)S(1)}, bf16[2,448,512]{2,1,0:T(8,128)(2,1)S(1)}, u32[]{:S(2)}, u32[]{:S(2)}) collective-permute-start(bf16[2,448,512]{2,1,0:T(8,128)(2,1)S(1)} %get-tuple-element.82), channel_id=1, source_target_pairs={{0,16},{16,32},{32,48},{48,0},{1,17},{17,33},{33,49},{49,1},{2,18}... | collective-permute-start | bytes 2752520 | tf_op jit(solution)/shard_map/ppermute | solution.py:22
  161.0 43.0 %collective-permute-start.7 = (bf16[2,448,512]{2,1,0:T(8,128)(2,1)S(1)}, bf16[2,448,512]{2,1,0:T(8,128)(2,1)S(1)}, u32[]{:S(2)}, u32[]{:S(2)}) collective-permute-start(bf16[2,448,512]{2,1,0:T(8,128)(2,1)S(1)} %get-tuple-element.82), channel_id=1, source_target_pairs={{0,48},{16,0},{32,16},{48,32},{1,49},{17,1},{33,17},{49,33},{2,50}... | collective-permute-start | bytes 2752520 | tf_op jit(solution)/shard_map/ppermute | solution.py:22
  203.9 13.1 %collective-permute-start.9 = (bf16[448,512]{1,0:T(8,128)(2,1)S(1)}, bf16[448,512]{1,0:T(8,128)(2,1)S(1)}, u32[]{:S(2)}, u32[]{:S(2)}) collective-permute-start(bf16[448,512]{1,0:T(8,128)(2,1)S(1)} %slice_bitcast_fusion.7), channel_id=1, source_target_pairs={{0,16},{16,32},{32,48},{48,0},{1,17},{17,33},{33,49},{49,1},{2,18}... | collective-permute-start | bytes 1376264 | tf_op jit(solution)/shard_map/ppermute | solution.py:22
  204.1 12.9 %collective-permute-start.10 = (bf16[448,512]{1,0:T(8,128)(2,1)S(1)}, bf16[448,512]{1,0:T(8,128)(2,1)S(1)}, u32[]{:S(2)}, u32[]{:S(2)}) collective-permute-start(bf16[448,512]{1,0:T(8,128)(2,1)S(1)} %slice_bitcast_fusion.6), channel_id=1, source_target_pairs={{0,48},{16,0},{32,16},{48,32},{1,49},{17,1},{33,17},{49,33},{2,50}... | collective-permute-start | bytes 1376264 | tf_op jit(solution)/shard_map/ppermute | solution.py:22
  256.9 87.2 %reduce-scatter.6.cloned.1.call-start = ((), (), s32[]{:S(2)}) async-start(), calls=%async_computation.4 | async-start | bytes 4587520 | tf_op jit(solution)/shard_map/reduce_scatter | solution.py:267
  272.6 30.4 %collective-permute-start.22 = (bf16[4,512,256]{2,1,0:T(8,128)(2,1)}, bf16[4,512,256]{2,1,0:T(8,128)(2,1)S(1)}, u32[]{:S(2)}, u32[]{:S(2)}) collective-permute-start(bf16[4,512,256]{2,1,0:T(8,128)(2,1)} %get-tuple-element.66), channel_id=1, source_target_pairs={{0,2},{2,4},{4,6},{6,0},{1,3},{3,5},{5,7},{7,1},{8,10},{10,12},{12... | collective-permute-start | bytes 3145736 | tf_op jit(solution)/shard_map/ppermute | solution.py:22
  274.4 48.5 %collective-permute-start.23 = (bf16[4,512,256]{2,1,0:T(8,128)(2,1)}, bf16[4,512,256]{2,1,0:T(8,128)(2,1)}, u32[]{:S(2)}, u32[]{:S(2)}) collective-permute-start(bf16[4,512,256]{2,1,0:T(8,128)(2,1)} %get-tuple-element.65), channel_id=1, source_target_pairs={{0,4},{2,6},{4,0},{6,2},{1,5},{3,7},{5,1},{7,3},{8,12},{10,14},{12... | collective-permute-start | bytes 3145736 | tf_op jit(solution)/shard_map/ppermute | solution.py:22
  276.6 46.4 %collective-permute-start.24 = (bf16[4,512,256]{2,1,0:T(8,128)(2,1)}, bf16[4,512,256]{2,1,0:T(8,128)(2,1)}, u32[]{:S(2)}, u32[]{:S(2)}) collective-permute-start(bf16[4,512,256]{2,1,0:T(8,128)(2,1)} %get-tuple-element.64), channel_id=1, source_target_pairs={{0,6},{2,0},{4,2},{6,4},{1,7},{3,1},{5,3},{7,5},{8,14},{10,8},{12,... | collective-permute-start | bytes 3145736 | tf_op jit(solution)/shard_map/ppermute | solution.py:22
  280.1 42.9 %collective-permute-start.25 = (bf16[448,512]{1,0:T(8,128)(2,1)}, bf16[448,512]{1,0:T(8,128)(2,1)}, u32[]{:S(2)}, u32[]{:S(2)}) collective-permute-start(bf16[448,512]{1,0:T(8,128)(2,1)} %get-tuple-element.72), channel_id=1, source_target_pairs={{0,64},{64,0},{1,65},{65,1},{2,66},{66,2},{3,67},{67,3},{4,68},{68... | collective-permute-start | bytes 1376264 | tf_op jit(solution)/shard_map/ppermute | solution.py:22
  301.5 42.7 %collective-permute-start.29 = (bf16[2,448,512]{2,1,0:T(8,128)(2,1)}, bf16[2,448,512]{2,1,0:T(8,128)(2,1)S(1)}, u32[]{:S(2)}, u32[]{:S(2)}) collective-permute-start(bf16[2,448,512]{2,1,0:T(8,128)(2,1)} %multiply_bitcast_fusion), channel_id=1, source_target_pairs={{0,64},{64,0},{1,65},{65,1},{2,66},{66,2},{3,67},{67,3},{4,68},{68... | collective-permute-start | bytes 2752520 | tf_op jit(solution)/shard_map/ppermute | solution.py:22
  327.7 14.5 %collective-permute-start.27 = (bf16[512,256]{1,0:T(8,128)(2,1)}, bf16[512,256]{1,0:T(8,128)(2,1)}, u32[]{:S(2)}, u32[]{:S(2)}) collective-permute-start(bf16[512,256]{1,0:T(8,128)(2,1)} %get-tuple-element.70), channel_id=1, source_target_pairs={{0,8},{64,72},{8,0},{72,64},{1,9},{65,73},{9,1},{73,65},{2,10},{66... | collective-permute-start | bytes 786440 | tf_op jit(solution)/shard_map/ppermute | solution.py:22
  330.4 11.8 %collective-permute-start.28 = (bf16[512,256]{1,0:T(8,128)(2,1)}, bf16[512,256]{1,0:T(8,128)(2,1)}, u32[]{:S(2)}, u32[]{:S(2)}) collective-permute-start(bf16[512,256]{1,0:T(8,128)(2,1)} %get-tuple-element.69), channel_id=1, source_target_pairs={{0,72},{64,0},{8,64},{72,8},{1,73},{65,1},{9,65},{73,9},{2,74},{66... | collective-permute-start | bytes 786440 | tf_op jit(solution)/shard_map/ppermute | solution.py:22
  (10 other events, 94.6 us)
Sparse Core Ops, SparseCore 0:
  14.9 46.5 all-gather.6
  63.7 44.1 all-gather.4
  146.2 62.2 reduce-scatter.3
  257.0 42.2 reduce-scatter.7
  301.6 42.3 reduce-scatter.5
